TPU v7x, 32 devices: a whole 2x2x4 slice. The times are simulated.
32 devices in a mesh: sub: 2 (over x), col: 8 (over z, core), grp: 2 (over y).
Axes of the slice: x: 2, y: 2, z: 4, core: 2. Of those that a mesh axis runs over, the one named last changes fastest.
Arguments:
- first_rhs: float32 [2, 640, 1024], P('sub', None, 'col'), may hold values from -6 to 6
- innovations: float32 [2, 512, 640], P('sub', 'col'), may hold values from -6 to 6
- start_mult: float32 [2, 640, 1024], P('sub', None, 'col'), may hold values from -4 to 4
- trajectory: bfloat16 [2, 640, 1024], P('sub', None, 'col'), may hold values from -6 to 6
- weight_in: float32 [4096, 640], P('grp'), may hold values from -0.25 to 0.25
- weight_out: float32 [640, 4096], P(None, 'grp'), may hold values from -0.09375 to 0.09375
- vertical_modes: float32 [640, 640], P('grp'), may hold values from -0.25 to 0.25
- length_scale: float32 [640], replicated, may hold values from 1 to 8
- band_limit: int32 [640], replicated, may hold values from 1 to 128
- obs_col: int32 [2, 512], P('sub', 'col'), may hold values from 0 to 1023, as said below
- obs_count: int32 [2, 8], P('sub', 'col'), may hold values from 1 to 64
- obs_var: float32 [2, 512], P('sub', 'col'), may hold values from 0.25 to 4
Outputs:
- multiplier: float32 [2, 640, 1024], P('sub', None, 'col')
- obs_multiplier: float32 [2, 512, 640], P('sub', 'col')
- increment: float32 [2, 640, 1024], P('sub', None, 'col')
Inputs may be any that keep to these rules, and one draw needn't show every extreme that they name: `obs_col`: slot j of a subwindow observes a column of shard j // 64: a column from (j // 64) * 128 to (j // 64 + 1) * 128 - 1.
All inputs are finite; a program needn't handle non-finite values.
Results may differ from a plain program's by a relative error of at most 0.0003.
Values sent between devices are 32-bit elements; how exact they have to be, the bound alone decides.
No kernel may reach another device: no remote copies, remote signals or barrier semaphores. Data moves between devices by JAX's collectives and lax.ppermute only.
A program may use at most 128 MiB of HBM per device.

v0:
```python
import math

import jax
import jax.numpy as jnp
import numpy as np
from jax import lax
from jax.sharding import PartitionSpec as P

KW = 128


HIGH = lax.Precision.HIGH


def contract(left, right, over):
    return lax.dot_general(
        left, right, ((over[:1], over[1:]), ((), ())), precision=HIGH, preferred_element_type=jnp.float32
    )


def product(left, right):
    return contract(left, right, (1, 0))


def product_first(left, right):
    return contract(left, right, (0, 0))


def spectral_table(columns, count, total):
    waves = jnp.arange(count, dtype=jnp.int32)
    phase = columns[:, None] * waves[None, :] % total
    angle = 2.0 * math.pi / total * phase.astype(jnp.float32)
    return jnp.concatenate([jnp.cos(angle), jnp.sin(angle)], axis=1)


def spectrum(scales, limits, total, count):
    waves = jnp.arange(count, dtype=jnp.int32)
    wavef = waves.astype(jnp.float32)
    decay = jnp.exp(-0.5 * (2.0 * math.pi * wavef[None, :] * scales[:, None] / total) ** 2)
    factor = jnp.where(waves == 0, 1.0, 2.0).astype(jnp.float32) / total
    keep = (waves[None, :] < limits[:, None]).astype(jnp.float32)
    values = decay * factor[None, :] * keep
    return jnp.concatenate([values, values], axis=1)


def rotated(block, axis, distance):
    size = lax.axis_size(axis)
    return lax.ppermute(block, axis, [(i, (i + distance) % size) for i in range(size)])


def mixtures(field, plans):
    size = lax.axis_size("sub")
    here = lax.axis_index("sub")
    masked = []
    for matrix, unread, zero in plans:
        weights = np.array(matrix, dtype=np.float32)
        live = np.ones_like(weights, dtype=bool)
        live[list(unread), :] = False
        live[:, list(zero)] = False
        masked.append((weights, live))
    arrived = {}
    for distance in range(1, size):
        route = [
            (source, (source + distance) % size)
            for source in range(size)
            if any(w[(source + distance) % size, source] * l[(source + distance) % size, source] for w, l in masked)
        ]
        if route:
            arrived[distance] = lax.ppermute(field, "sub", route)
    results = []
    for weights, live in masked:
        total = None
        for distance in range(size):
            cells = [(i, (i - distance) % size) for i in range(size)]
            used = {float(weights[c]) for c in cells if live[c]}
            if not used or used == {0.0}:
                continue
            block = field if distance == 0 else arrived[distance]
            if len(used) > 1:
                block = block * jnp.asarray([weights[c] for c in cells], jnp.float32)[here]
            elif used != {1.0}:
                block = block * used.pop()
            total = block if total is None else total + block
        results.append(total)
    return results


def plus(*terms):
    kept = [term for term in terms if term is not None]
    return sum(kept[1:], kept[0]) if kept else None


def on_device(
    first_rhs,
    innovations,
    start_mult,
    trajectory,
    weight_in,
    weight_out,
    vertical_modes,
    length_scale,
    band_limit,
    obs_col,
    obs_count,
    obs_var,
):
    rhs = first_rhs[0]
    data = innovations[0]
    start = start_mult[0]
    variance = obs_var[0][:, None]
    depth, width = rhs.shape
    subs = lax.axis_size("sub")
    shards = lax.axis_size("col")
    groups = lax.axis_size("grp")
    here = lax.axis_index("sub")
    column_index = lax.axis_index("col")
    group_index = lax.axis_index("grp")
    total_cols = width * shards
    half_modes = vertical_modes.shape[0]
    owned_modes = half_modes // shards
    rows = depth // groups

    ones = np.ones((subs, subs))
    up = np.eye(subs, k=1)
    down = np.eye(subs, k=-1)
    later = np.triu(ones)
    earlier = np.tril(ones)
    first = (0,)

    def own(field):
        return lax.dynamic_slice_in_dim(field, group_index * rows, rows, 0)

    def summed(partial):
        return sum((rotated(partial, "grp", step) for step in range(1, groups)), partial)

    def summed_own(partial):
        total = own(partial)
        for step in range(1, groups):
            target = (group_index + step) % groups
            total = total + rotated(
                lax.dynamic_slice_in_dim(partial, target * rows, rows, 0), "grp", step
            )
        return total

    def joined(block):
        whole = lax.dynamic_update_slice_in_dim(
            jnp.zeros((depth, block.shape[1]), block.dtype), block, group_index * rows, 0
        )
        for step in range(1, groups):
            source = (group_index - step) % groups
            whole = lax.dynamic_update_slice_in_dim(whole, rotated(block, "grp", step), source * rows, 0)
        return whole

    before = lax.ppermute(trajectory[0].astype(jnp.float32), "sub", [(i, i + 1) for i in range(subs - 1)])
    slopes = (1.0 - jnp.tanh(product(weight_in, before)) ** 2) * (here > 0).astype(jnp.float32)

    def side_by_side(*fields):
        return jnp.concatenate(fields, axis=1)

    def scaled(inner):
        return inner * jnp.tile(slopes, (1, inner.shape[1] // width))

    def tangent(fields):
        return product(weight_out, scaled(product(weight_in, fields)))

    def adjoint(fields):
        return product_first(weight_in, scaled(product_first(weight_out, fields)))

    first_mode = group_index * half_modes + column_index * owned_modes
    owned_scales = lax.dynamic_slice_in_dim(length_scale, first_mode, owned_modes, 0)
    owned_limits = lax.dynamic_slice_in_dim(band_limit, first_mode, owned_modes, 0)
    owned_spec = spectrum(owned_scales, owned_limits, total_cols, KW)
    table = spectral_table(jnp.arange(total_cols, dtype=jnp.int32), KW, total_cols)
    table_blocks = table.reshape(shards, width, 2 * KW)

    def covariance(fields):
        count = fields.shape[1] // width
        amplitudes = product(vertical_modes, fields).reshape(shards, owned_modes, count, width)
        owned = lax.all_to_all(amplitudes, "col", 0, 0, tiled=True)
        owned = owned.transpose(1, 2, 0, 3).reshape(owned_modes * count, total_cols)
        coeffs = product(owned, table).reshape(owned_modes, count, 2 * KW) * owned_spec[:, None, :]
        back = contract(coeffs.reshape(owned_modes * count, 2 * KW), table, (1, 1))
        back = back.reshape(owned_modes, count, shards, width).transpose(2, 0, 1, 3)
        returned = lax.all_to_all(back, "col", 0, 0, tiled=True)
        return product_first(vertical_modes, returned.reshape(half_modes, count * width))

    local_cols = obs_col[0] - column_index * width
    slot_ids = jnp.arange(local_cols.shape[0], dtype=jnp.int32)
    live = (slot_ids < obs_count[0, 0]).astype(jnp.float32)
    pick = (jnp.arange(width, dtype=jnp.int32)[:, None] == local_cols[None, :]).astype(jnp.float32) * live[None, :]

    def observe(field):
        return contract(pick, field, (0, 1))

    def spread(values):
        return contract(values, pick, (0, 1))

    dir_obs = data / variance
    obs_push = spread(dir_obs)

    push_fed, push_later = mixtures(obs_push, [(later, first, ()), (later, (), ())])
    pulled = adjoint(side_by_side(start, push_fed))
    pull0 = summed(pulled[:, :width])
    pull2 = summed_own(pulled[:, width:])
    pull0_fed, pull0_later = mixtures(pull0, [(later @ up, first, first), (later @ up, (), first)])
    pull1 = pull1_later = None
    if pull0_fed is not None:
        pull1 = summed(adjoint(pull0_fed))
        pull1_fed, pull1_later = mixtures(pull1, [(later @ up, first, first), (later @ up, (), first)])
        pull2 = pull2 + own(summed(adjoint(pull0_fed - pull1_fed)))

    early = covariance(side_by_side(start, obs_push))
    cov_start = summed_own(early[:, :width])
    cov_push = summed(early[:, width:])
    push_feed, push_state = mixtures(
        cov_push, [(down @ earlier @ later, first, ()), (earlier @ later, (), ())]
    )
    rhs_feed, rhs_state = mixtures(rhs, [(down @ earlier, first, ()), (earlier, (), ())])
    fed = tangent(side_by_side(rhs_feed, push_feed))
    fed_rhs = summed_own(fed[:, :width])
    fed_push = summed_own(fed[:, width:])

    cov_pull = summed(covariance(pull0))
    pull_feed, pull_state = mixtures(
        cov_pull, [(down @ earlier @ later @ up, first, first), (earlier @ later @ up, (), first)]
    )
    fed_pull = summed_own(tangent(pull_feed))

    dir_mult = pull0_later - start
    dir_state = rhs_state - pull_state
    moved = fed_rhs - fed_pull
    moved_turn = fed_pull + fed_push
    moved_whole = joined(moved)
    turn_mult = plus(pull0_later, push_later)
    if pull1 is not None:
        turn_mult = turn_mult - pull1_later
        cov_pull1 = summed(covariance(pull1))
        pull1_feed, pull1_state = mixtures(
            cov_pull1, [(down @ earlier @ later @ up, first, first), (earlier @ later @ up, (), first)]
        )
        pull_state = pull_state - pull1_state
        moved_turn = moved_turn - summed_own(tangent(pull1_feed))
    moved_feed, moved_state = mixtures(moved_whole, [(down @ earlier, first, first), (earlier, (), first)])
    if moved_feed is not None:
        moved_turn = moved_turn + summed_own(tangent(moved_feed))
    turn_state = moved_state + pull_state + push_state

    own_start = own(start)
    own_push = own(obs_push)
    own_pull = own(pull0)
    res1 = own(rhs) - cov_start
    image1 = res1 - moved
    turn1 = image1 - moved + moved_turn
    seen = observe(dir_state)
    own_data = lax.dynamic_slice_in_dim(data, group_index * rows, rows, 1)
    own_seen = lax.dynamic_slice_in_dim(seen, group_index * rows, rows, 1)
    image2 = own_data + own_seen
    turn2 = image2 + own_seen - observe(own(turn_state))
    (from_next,) = mixtures(own_start, [(up, (), ())])
    (pull_next,) = mixtures(own_pull, [(up, (), first)])
    (pull2_next,) = mixtures(pull2, [(up, (), first)])
    res3 = from_next - own_start + pull_next
    image3 = res3 + pull_next + own_push
    turn3 = image3 + pull_next - pull2_next + own_push + spread(own_seen / variance)
    if pull1 is not None:
        (pull1_next,) = mixtures(own(pull1), [(up, (), first)])
        image3 = image3 - pull1_next
        turn3 = turn3 - 2.0 * pull1_next

    def dot(left, right):
        return sum(jnp.sum(a * b) for a, b in zip(left, right))

    res = (res1, own_data, res3)
    image = (image1, image2, image3)
    turn = (turn1, turn2, turn3)
    sums = jnp.stack(
        [dot(image, res), dot(image, image), dot(turn, res), dot(turn, image), dot(turn, turn)]
    )
    sums = jnp.zeros((8, 128), jnp.float32).at[0, :5].set(sums)
    for axis in ("col", "grp", "sub"):
        size = lax.axis_size(axis)
        step = 1
        while step < size:
            sums = sums + lax.ppermute(sums, axis, [(i, i ^ step) for i in range(size)])
            step *= 2
    upper, square, turn_res, turn_image, turn_square = (sums[0, i] for i in range(5))
    alpha = upper / square
    alpha_next = (upper - alpha * square - alpha * (turn_res - alpha * turn_image)) / (
        square - 2.0 * alpha * turn_image + alpha * alpha * turn_square
    )
    keep = alpha + alpha_next * (1.0 - alpha)
    mixed = alpha * alpha_next
    multiplier = start + keep * dir_mult - mixed * turn_mult
    obs_multiplier = (alpha + alpha_next) * dir_obs - mixed * ((data + seen) / variance)
    increment = keep * dir_state + mixed * turn_state
    return (multiplier[None], obs_multiplier[None], increment[None])


def solution(mesh):
    placed = (
        P("sub", None, "col"),
        P("sub", "col", None),
        P("sub", None, "col"),
        P("sub", None, "col"),
        P("grp", None),
        P(None, "grp"),
        P("grp", None),
        P(),
        P(),
        P("sub", "col"),
        P("sub", "col"),
        P("sub", "col"),
    )
    return jax.shard_map(
        on_device,
        mesh=mesh,
        in_specs=placed,
        out_specs=(P("sub", None, "col"), P("sub", "col", None), P("sub", None, "col")),
        check_vma=False,
    )
```

profile of v0, /device:TPU:0, one launch (start us, length us, event | category | flops | bytes accessed | tf_op | source)
XLA Modules:
  0.0 203.3 jit_solution(15566572235542702363)
XLA Ops:
  1.7 4.9 %collective-permute-start.4 = (f32[640,128]{1,0:T(8,128)S(1)}, f32[640,128]{1,0:T(8,128)S(1)}, u32[]{:S(2)}, u32[]{:S(2)}) collective-permute-start(f32[640,128]{1,0:T(8,128)S(1)} %bitcast_convert_fusion), channel_id=1, source_target_pairs={{0,16},{1,17},{2,18},{3,19},{4,20},{5,21},{6,22},{7,23},{8,24},{9,... | collective-permute-start | bytes 983048 | tf_op jit(solution)/shard_map/ppermute | solution.py:154
  12.6 4.9 %all-to-all-start = ((f32[8,40,2,128]{3,1,2,0:T(8,128)}), f32[8,40,2,128]{3,1,2,0:T(8,128)}, u32[]{:S(2)}, u32[]{:S(2)}) async-start(f32[8,40,2,128]{3,1,2,0:T(8,128)} %copy.36), calls=%async_computation | async-start | bytes 655360 | tf_op jit(solution)/shard_map/all_to_all | solution.py:179
  17.4 2.0 collective-permute-start.1
  22.4 2.9 %fusion.40 = (f32[1024,128]{1,0:T(8,128)}, f32[1024,128]{1,0:T(8,128)}) fusion(), kind=kLoop, calls=%fused_computation.72 | loop fusion | flops 1835008 | bytes 1048576 | tf_op jit(solution)/shard_map/sin | solution.py:33
  28.7 3.2 %fusion.39 = (f32[8,128,128]{2,1,0:T(8,128)}, f32[8,128,128]{2,1,0:T(8,128)}) fusion(s32[8,128]{1,0:T(8,128)S(1)} %multiply_add_fusion), kind=kLoop, calls=%fused_computation.71 | loop fusion | flops 1835008 | bytes 1052672 | tf_op jit(solution)/shard_map/cos | solution.py:33
  32.0 5.7 %fusion.3 = f32[2048,128]{1,0:T(8,128)} fusion(f32[2048,640]{1,0:T(8,128)} %param.22, f32[640,128]{1,0:T(8,128)S(1)} %collective-permute-done.4, f32[]{:T(128)S(6)} %convert_element_type.57), kind=kOutput, calls=%fused_computation.9 | convolution fusion | flops 1007419392 | bytes 6619140 | tf_op jit(solution)/shard_map/dot_general | solution.py:16
  39.3 4.9 %bitcast_multiply_fusion = f32[2048,256]{0,1:T(8,128)S(1)} fusion(f32[640,2048]{1,0:T(8,128)} %param.23, f32[2048,128]{0,1:T(8,128)S(1)} %copy.41, f32[640,128]{1,0:T(8,128)} %copy-done.5, f32[640,128]{1,0:T(8,128)S(1)} %bitcast.175), kind=kOutput, calls=%fused_computation | convolution fusion | flops 2013954048 | bytes 9043968 | tf_op jit(solution)/shard_map/dot_general | solution.py:16
  44.3 4.2 %convolution_bitcast_fusion.3 = f32[640,256]{1,0:T(8,128)S(1)} fusion(f32[2048,256]{0,1:T(8,128)S(1)} %bitcast_multiply_fusion, f32[2048,640]{1,0:T(8,128)S(1)} %bitcast.169), kind=kOutput, calls=%fused_computation.10 | convolution fusion | flops 2013265920 | bytes 7995392 | tf_op jit(solution)/shard_map/dot_general | solution.py:16
  50.3 8.5 %collective-permute-done.6 = f32[640,128]{1,0:T(8,128)S(1)} collective-permute-done((f32[640,128]{1,0:T(8,128)S(1)}, f32[640,128]{1,0:T(8,128)S(1)}, u32[]{:S(2)}, u32[]{:S(2)}) %collective-permute-start.6) | collective-permute-done | bytes 327712 | tf_op jit(solution)/shard_map/ppermute | solution.py:48
  61.5 4.7 %all-to-all-start.2 = ((f32[8,40,1,128]{3,1,2,0:T(8,128)}), f32[8,40,1,128]{3,1,2,0:T(8,128)S(1)}, u32[]{:S(2)}, u32[]{:S(2)}) async-start(f32[8,40,1,128]{3,1,2,0:T(8,128)} %bitcast.23), calls=%async_computation.2 | async-start | bytes 327680 | tf_op jit(solution)/shard_map/all_to_all | solution.py:179
  67.9 1.8 convolution_bitcast_fusion.7
  70.5 2.9 %all-to-all-done.2 = f32[8,40,1,128]{3,1,2,0:T(8,128)S(1)} async-done(((f32[8,40,1,128]{3,1,2,0:T(8,128)}), f32[8,40,1,128]{3,1,2,0:T(8,128)S(1)}, u32[]{:S(2)}, u32[]{:S(2)}) %all-to-all-start.2) | async-done | bytes 163872 | tf_op jit(solution)/shard_map/all_to_all | solution.py:179
  73.4 4.3 %all-to-all-start.1 = ((f32[8,40,2,128]{3,1,2,0:T(8,128)}), f32[8,40,2,128]{3,1,2,0:T(8,128)}, u32[]{:S(2)}, u32[]{:S(2)}) async-start(f32[8,40,2,128]{3,1,2,0:T(8,128)} %copy.38), calls=%async_computation.1 | async-start | bytes 655360 | tf_op jit(solution)/shard_map/all_to_all | solution.py:184
  77.6 2.1 %fusion.37 = (f32[1,8,128,128]{3,2,1,0:T(8,128)S(1)}, f32[1,8,128,128]{3,2,1,0:T(8,128)S(1)}) fusion(s32[8,128]{1,0:T(8,128)S(1)} %multiply_add_fusion), kind=kLoop, calls=%fused_computation.69 | loop fusion | flops 1835008 | bytes 1052672 | tf_op jit(solution)/shard_map/cos | solution.py:33
  83.1 5.5 %all-to-all-done.1 = f32[8,40,2,128]{3,1,2,0:T(8,128)} async-done(((f32[8,40,2,128]{3,1,2,0:T(8,128)}), f32[8,40,2,128]{3,1,2,0:T(8,128)}, u32[]{:S(2)}, u32[]{:S(2)}) %all-to-all-start.1) | async-done | bytes 327712 | tf_op jit(solution)/shard_map/all_to_all | solution.py:184
  88.6 3.5 %all-to-all-start.3 = ((f32[8,40,1,128]{3,1,2,0:T(8,128)}), f32[8,40,1,128]{3,1,2,0:T(8,128)S(1)}, u32[]{:S(2)}, u32[]{:S(2)}) async-start(f32[8,40,1,128]{3,1,2,0:T(8,128)} %convolution_bitcast_fusion.9), calls=%async_computation.3 | async-start | bytes 327680 | tf_op jit(solution)/shard_map/all_to_all | solution.py:184
  105.0 6.1 %collective-permute-done.2 = f32[640,128]{1,0:T(8,128)} collective-permute-done((f32[640,128]{1,0:T(8,128)}, f32[640,128]{1,0:T(8,128)}, u32[]{:S(2)}, u32[]{:S(2)}) %collective-permute-start.2) | collective-permute-done | bytes 327712 | tf_op jit(solution)/shard_map/ppermute | solution.py:48
  113.6 3.5 %collective-permute-done.7 = f32[640,128]{1,0:T(8,128)S(1)} collective-permute-done((f32[640,128]{1,0:T(8,128)S(1)}, f32[640,128]{1,0:T(8,128)S(1)}, u32[]{:S(2)}, u32[]{:S(2)}) %collective-permute-start.7) | collective-permute-done | bytes 327712 | tf_op jit(solution)/shard_map/ppermute | solution.py:48
  117.2 3.7 %collective-permute-start.3 = (f32[640,128]{1,0:T(8,128)S(1)}, f32[640,128]{1,0:T(8,128)S(1)}, u32[]{:S(2)}, u32[]{:S(2)}) collective-permute-start(f32[640,128]{1,0:T(8,128)S(1)} %get-tuple-element.42), channel_id=1, source_target_pairs={{0,16},{16,0},{1,17},{17,1},{2,18},{18,2},{3,19},{19,3},{4,20},{20... | collective-permute-start | bytes 983048 | tf_op jit(solution)/shard_map/ppermute | solution.py:69
  120.9 5.3 %fusion = f32[2048,128]{1,0:T(8,128)S(1)} fusion(f32[2048,128]{1,0:T(8,128)} %fusion.3, f32[640,128]{1,0:T(8,128)S(1)} %add.256, f32[2048,640]{1,0:T(8,128)} %param.22), kind=kOutput, calls=%fused_computation.5 | convolution fusion | flops 1006895104 | bytes 7667712 | tf_op jit(solution)/shard_map/dot_general | solution.py:16
  126.2 2.2 %fusion.97 = f32[128,640]{0,1:T(8,128)S(1)} fusion(f32[2048,128]{1,0:T(8,128)S(1)} %fusion, f32[640,2048]{1,0:T(8,128)S(1)} %bitcast.173), kind=kOutput, calls=%fused_computation.174 | convolution fusion | flops 1006632960 | bytes 6619136 | tf_op jit(solution)/shard_map/dot_general | solution.py:16
  129.1 5.3 %bitcast_multiply_fusion.1 = f32[2048,256]{0,1:T(8,128)S(1)} fusion(f32[2048,640]{1,0:T(8,128)S(1)} %bitcast.171, f32[2048,128]{0,1:T(8,128)S(1)} %copy.41, f32[640,128]{1,0:T(8,128)S(1)} %add.252, f32[640,128]{1,0:T(8,128)} %collective-permute-done.1), kind=kOutput, calls=%fused_computation.1 | convolution fusion | flops 2013954048 | bytes 9043968 | tf_op jit(solution)/shard_map/dot_general | solution.py:16
  134.5 2.2 %convolution_bitcast_fusion.4 = f32[640,256]{1,0:T(8,128)S(1)} fusion(f32[2048,256]{0,1:T(8,128)S(1)} %bitcast_multiply_fusion.1, f32[640,2048]{1,0:T(8,128)S(1)} %bitcast.173), kind=kOutput, calls=%fused_computation.11 | convolution fusion | flops 2013265920 | bytes 7995392 | tf_op jit(solution)/shard_map/dot_general | solution.py:16
  139.1 4.9 %collective-permute-done.5 = f32[320,128]{1,0:T(8,128)S(1)} collective-permute-done((f32[320,128]{1,0:T(8,128)S(1)}, f32[320,128]{1,0:T(8,128)S(1)}, u32[]{:S(2)}, u32[]{:S(2)}) %collective-permute-start.5) | collective-permute-done | bytes 163872 | tf_op jit(solution)/shard_map/ppermute | solution.py:48
  151.7 3.0 %collective-permute-done.13 = f32[320,128]{1,0:T(8,128)S(1)} collective-permute-done((f32[320,128]{1,0:T(8,128)S(1)}, f32[320,128]{1,0:T(8,128)S(1)}, u32[]{:S(2)}, u32[]{:S(2)}) %collective-permute-start.13) | collective-permute-done | bytes 163872 | tf_op jit(solution)/shard_map/ppermute | solution.py:48
  155.9 2.4 %add_add_fusion = (f32[640,128]{1,0:T(8,128)S(1)}, f32[640,128]{1,0:T(8,128)S(1)}) fusion(f32[640,128]{1,0:T(8,128)S(1)} %collective-permute-done.3, f32[640,128]{1,0:T(8,128)S(1)} %get-tuple-element.42, f32[640,128]{1,0:T(8,128)S(1)} %constant_dynamic-update-slice_fusion, f32[]{:T(128)} %bitcast.41, f32[640,128]{1,0:T(8,128)S(1)} %add.256, ...), kind=kLoop, calls=%fused_computation.66 | loop fusion | flops 655360 | bytes 2949128 | tf_op jit(solution)/shard_map/add | solution.py:246
  174.7 2.2 %collective-permute-done.17 = f32[8,128]{1,0:T(8,128)S(1)} collective-permute-done((f32[8,128]{1,0:T(8,128)S(1)}, f32[8,128]{1,0:T(8,128)S(1)}, u32[]{:S(2)}, u32[]{:S(2)}) %collective-permute-start.17) | collective-permute-done | bytes 4128 | tf_op jit(solution)/shard_map/ppermute | solution.py:284
  177.0 2.3 %collective-permute-start.18 = (f32[8,128]{1,0:T(8,128)S(1)}, f32[8,128]{1,0:T(8,128)S(1)}, u32[]{:S(2)}, u32[]{:S(2)}) collective-permute-start(f32[8,128]{1,0:T(8,128)S(1)} %add.289), channel_id=1, source_target_pairs={{0,8},{2,10},{4,12},{6,14},{8,0},{10,2},{12,4},{14,6},{1,9},{3,11}... | collective-permute-start | bytes 12296 | tf_op jit(solution)/shard_map/ppermute | solution.py:284
  179.2 2.2 %collective-permute-done.18 = f32[8,128]{1,0:T(8,128)S(1)} collective-permute-done((f32[8,128]{1,0:T(8,128)S(1)}, f32[8,128]{1,0:T(8,128)S(1)}, u32[]{:S(2)}, u32[]{:S(2)}) %collective-permute-start.18) | collective-permute-done | bytes 4128 | tf_op jit(solution)/shard_map/ppermute | solution.py:284
  183.0 2.1 %collective-permute-done.19 = f32[8,128]{1,0:T(8,128)S(1)} collective-permute-done((f32[8,128]{1,0:T(8,128)S(1)}, f32[8,128]{1,0:T(8,128)S(1)}, u32[]{:S(2)}, u32[]{:S(2)}) %collective-permute-start.19) | collective-permute-done | bytes 4128 | tf_op jit(solution)/shard_map/ppermute | solution.py:284
  197.5 3.3 %collective-permute-done.21 = f32[640,128]{1,0:T(8,128)} collective-permute-done((f32[640,128]{1,0:T(8,128)S(1)}, f32[640,128]{1,0:T(8,128)}, u32[]{:S(2)}, u32[]{:S(2)}) %collective-permute-start.21) | collective-permute-done | bytes 327712 | tf_op jit(solution)/shard_map/ppermute | solution.py:69
  200.9 2.4 %subtract_bitcast_fusion = f32[1,640,128]{2,1,0:T(8,128)} fusion(f32[640,128]{1,0:T(8,128)} %collective-permute-done.21, f32[640,128]{1,0:T(8,128)S(1)} %copy-done.6, f32[640,128]{1,0:T(8,128)S(1)} %collective-permute-done.22, f32[]{:T(128)} %bitcast.38, f32[]{:T(128)S(6)} %mul.417, f32[]{:T(128)S(6)} %add.294, f32[1,640,128]{2,1,0:T(8,128)S(1)} %copy-done.1), kind=kLoop, calls=%fused_computation.65 | loop fusion | flops 655360 | bytes 1638412 | tf_op jit(solution)/shard_map/broadcast_in_dim | solution.py:296
  (141 shorter events, 67.0 us)
Async XLA Ops:
  0.7 27.5 %copy-start.12 = (f32[2]{0:T(128)S(1)}, f32[2]{0:T(128)}, u32[]{:S(2)}) copy-start(f32[2]{0:T(128)} %constant.128.clone) | copy-start | bytes 28
  1.7 30.3 %collective-permute-start.4 = (f32[640,128]{1,0:T(8,128)S(1)}, f32[640,128]{1,0:T(8,128)S(1)}, u32[]{:S(2)}, u32[]{:S(2)}) collective-permute-start(f32[640,128]{1,0:T(8,128)S(1)} %bitcast_convert_fusion), channel_id=1, source_target_pairs={{0,16},{1,17},{2,18},{3,19},{4,20},{5,21},{6,22},{7,23},{8,24},{9,... | collective-permute-start | bytes 983048 | tf_op jit(solution)/shard_map/ppermute | solution.py:154
  12.6 48.9 %all-to-all-start = ((f32[8,40,2,128]{3,1,2,0:T(8,128)}), f32[8,40,2,128]{3,1,2,0:T(8,128)}, u32[]{:S(2)}, u32[]{:S(2)}) async-start(f32[8,40,2,128]{3,1,2,0:T(8,128)} %copy.36), calls=%async_computation | async-start | bytes 655360 | tf_op jit(solution)/shard_map/all_to_all | solution.py:179
  17.4 111.6 %collective-permute-start.1 = (f32[640,128]{1,0:T(8,128)}, f32[640,128]{1,0:T(8,128)}, u32[]{:S(2)}, u32[]{:S(2)}) collective-permute-start(f32[640,128]{1,0:T(8,128)} %bitcast.177), channel_id=1, source_target_pairs={{0,16},{1,17},{2,18},{3,19},{4,20},{5,21},{6,22},{7,23},{8,24},{9,... | collective-permute-start | bytes 983048 | tf_op jit(solution)/shard_map/ppermute | solution.py:69
  21.1 140.3 %collective-permute-start.10 = (f32[320,128]{1,0:T(8,128)}, f32[320,128]{1,0:T(8,128)}, u32[]{:S(2)}, u32[]{:S(2)}) collective-permute-start(f32[320,128]{1,0:T(8,128)} %dynamic-slice_bitcast_fusion), channel_id=1, source_target_pairs={{16,0},{17,1},{18,2},{19,3},{20,4},{21,5},{22,6},{23,7},{24,8},{25... | collective-permute-start | bytes 491528 | tf_op jit(solution)/shard_map/ppermute | solution.py:69
  48.6 32.8 %copy-start.2 = (f32[1024,128]{1,0:T(8,128)S(1)}, f32[1024,128]{1,0:T(8,128)}, u32[]{:S(2)}) copy-start(f32[1024,128]{1,0:T(8,128)} %get-tuple-element.56) | copy-start | bytes 1572868
  48.6 32.8 %copy-start.3 = (f32[1024,128]{1,0:T(8,128)S(1)}, f32[1024,128]{1,0:T(8,128)}, u32[]{:S(2)}) copy-start(f32[1024,128]{1,0:T(8,128)} %get-tuple-element.57) | copy-start | bytes 1572868
  48.6 10.2 %collective-permute-start.6 = (f32[640,128]{1,0:T(8,128)S(1)}, f32[640,128]{1,0:T(8,128)S(1)}, u32[]{:S(2)}, u32[]{:S(2)}) collective-permute-start(f32[640,128]{1,0:T(8,128)S(1)} %slice.64), channel_id=1, source_target_pairs={{0,1},{1,0},{2,3},{3,2},{4,5},{5,4},{6,7},{7,6},{8,9},{9,8},{10,11... | collective-permute-start | bytes 983048 | tf_op jit(solution)/shard_map/ppermute | solution.py:48
  61.5 11.9 %all-to-all-start.2 = ((f32[8,40,1,128]{3,1,2,0:T(8,128)}), f32[8,40,1,128]{3,1,2,0:T(8,128)S(1)}, u32[]{:S(2)}, u32[]{:S(2)}) async-start(f32[8,40,1,128]{3,1,2,0:T(8,128)} %bitcast.23), calls=%async_computation.2 | async-start | bytes 327680 | tf_op jit(solution)/shard_map/all_to_all | solution.py:179
  73.4 15.2 %all-to-all-start.1 = ((f32[8,40,2,128]{3,1,2,0:T(8,128)}), f32[8,40,2,128]{3,1,2,0:T(8,128)}, u32[]{:S(2)}, u32[]{:S(2)}) async-start(f32[8,40,2,128]{3,1,2,0:T(8,128)} %copy.38), calls=%async_computation.1 | async-start | bytes 655360 | tf_op jit(solution)/shard_map/all_to_all | solution.py:184
  88.6 37.6 %slice-start.4 = ((s8[5242880]{0:T(1024)(128)(4,1)}), s8[1048576]{0:T(1024)(128)(4,1)S(1)}, s32[]{:S(2)}) async-start(s8[5242880]{0:T(1024)(128)(4,1)} %bitcast.172), calls=%async_computation.8 | async-start | bytes 2097152
  88.6 12.1 %all-to-all-start.3 = ((f32[8,40,1,128]{3,1,2,0:T(8,128)}), f32[8,40,1,128]{3,1,2,0:T(8,128)S(1)}, u32[]{:S(2)}, u32[]{:S(2)}) async-start(f32[8,40,1,128]{3,1,2,0:T(8,128)} %convolution_bitcast_fusion.9), calls=%async_computation.3 | async-start | bytes 327680 | tf_op jit(solution)/shard_map/all_to_all | solution.py:184
  93.7 8.0 %collective-permute-start.14 = (f32[320,128]{1,0:T(8,128)}, f32[320,128]{1,0:T(8,128)}, u32[]{:S(2)}, u32[]{:S(2)}) collective-permute-start(f32[320,128]{1,0:T(8,128)} %constant_dynamic-slice_fusion), channel_id=1, source_target_pairs={{0,1},{1,0},{2,3},{3,2},{4,5},{5,4},{6,7},{7,6},{8,9},{9,8},{10,11... | collective-permute-start | bytes 491528 | tf_op jit(solution)/shard_map/ppermute | solution.py:48
  95.2 66.1 %collective-permute-start.11 = (f32[320,128]{1,0:T(8,128)}, f32[320,128]{1,0:T(8,128)}, u32[]{:S(2)}, u32[]{:S(2)}) collective-permute-start(f32[320,128]{1,0:T(8,128)} %constant_dynamic-slice_fusion.2), channel_id=1, source_target_pairs={{16,0},{17,1},{18,2},{19,3},{20,4},{21,5},{22,6},{23,7},{24,8},{25... | collective-permute-start | bytes 491528 | tf_op jit(solution)/shard_map/ppermute | solution.py:69
  100.2 10.9 %collective-permute-start.2 = (f32[640,128]{1,0:T(8,128)}, f32[640,128]{1,0:T(8,128)}, u32[]{:S(2)}, u32[]{:S(2)}) collective-permute-start(f32[640,128]{1,0:T(8,128)} %slice.62), channel_id=1, source_target_pairs={{0,1},{1,0},{2,3},{3,2},{4,5},{5,4},{6,7},{7,6},{8,9},{9,8},{10,11... | collective-permute-start | bytes 983048 | tf_op jit(solution)/shard_map/ppermute | solution.py:48
  101.7 15.4 %collective-permute-start.7 = (f32[640,128]{1,0:T(8,128)S(1)}, f32[640,128]{1,0:T(8,128)S(1)}, u32[]{:S(2)}, u32[]{:S(2)}) collective-permute-start(f32[640,128]{1,0:T(8,128)S(1)} %convolution_bitcast_fusion.6), channel_id=1, source_target_pairs={{0,1},{1,0},{2,3},{3,2},{4,5},{5,4},{6,7},{7,6},{8,9},{9,8},{10,11... | collective-permute-start | bytes 983048 | tf_op jit(solution)/shard_map/ppermute | solution.py:48
  111.1 50.2 %collective-permute-start.15 = (f32[320,128]{1,0:T(8,128)}, f32[320,128]{1,0:T(8,128)S(1)}, u32[]{:S(2)}, u32[]{:S(2)}) collective-permute-start(f32[320,128]{1,0:T(8,128)} %dynamic-slice_add_fusion), channel_id=1, source_target_pairs={{16,0},{17,1},{18,2},{19,3},{20,4},{21,5},{22,6},{23,7},{24,8},{25... | collective-permute-start | bytes 491528 | tf_op jit(solution)/shard_map/ppermute | solution.py:69
  117.2 11.3 %collective-permute-start.3 = (f32[640,128]{1,0:T(8,128)S(1)}, f32[640,128]{1,0:T(8,128)S(1)}, u32[]{:S(2)}, u32[]{:S(2)}) collective-permute-start(f32[640,128]{1,0:T(8,128)S(1)} %get-tuple-element.42), channel_id=1, source_target_pairs={{0,16},{16,0},{1,17},{17,1},{2,18},{18,2},{3,19},{19,3},{4,20},{20... | collective-permute-start | bytes 983048 | tf_op jit(solution)/shard_map/ppermute | solution.py:69
  128.5 10.0 %collective-permute-start.8 = (f32[320,128]{1,0:T(8,128)S(1)}, f32[320,128]{1,0:T(8,128)S(1)}, u32[]{:S(2)}, u32[]{:S(2)}) collective-permute-start(f32[320,128]{1,0:T(8,128)S(1)} %dynamic-slice_bitcast_fusion.1), channel_id=1, source_target_pairs={{0,1},{1,0},{2,3},{3,2},{4,5},{5,4},{6,7},{7,6},{8,9},{9,8},{10,11... | collective-permute-start | bytes 491528 | tf_op jit(solution)/shard_map/ppermute | solution.py:48
  136.8 7.1 %collective-permute-start.5 = (f32[320,128]{1,0:T(8,128)S(1)}, f32[320,128]{1,0:T(8,128)S(1)}, u32[]{:S(2)}, u32[]{:S(2)}) collective-permute-start(f32[320,128]{1,0:T(8,128)S(1)} %constant_dynamic-slice_fusion.3), channel_id=1, source_target_pairs={{0,1},{1,0},{2,3},{3,2},{4,5},{5,4},{6,7},{7,6},{8,9},{9,8},{10,11... | collective-permute-start | bytes 491528 | tf_op jit(solution)/shard_map/ppermute | solution.py:48
  138.4 48.6 %copy-start.8 = (f32[640,128]{1,0:T(8,128)S(1)}, f32[640,128]{1,0:T(8,128)}, u32[]{:S(2)}) copy-start(f32[640,128]{1,0:T(8,128)} %copy-done.7) | copy-start | bytes 983044
  138.5 8.5 %collective-permute-start = (f32[320,128]{1,0:T(8,128)S(1)}, f32[320,128]{1,0:T(8,128)S(1)}, u32[]{:S(2)}, u32[]{:S(2)}) collective-permute-start(f32[320,128]{1,0:T(8,128)S(1)} %constant_dynamic-slice_fusion.4), channel_id=1, source_target_pairs={{0,1},{1,0},{2,3},{3,2},{4,5},{5,4},{6,7},{7,6},{8,9},{9,8},{10,11... | collective-permute-start | bytes 491528 | tf_op jit(solution)/shard_map/ppermute | solution.py:48
  144.0 5.4 %collective-permute-start.12 = (f32[320,128]{1,0:T(8,128)S(1)}, f32[320,128]{1,0:T(8,128)S(1)}, u32[]{:S(2)}, u32[]{:S(2)}) collective-permute-start(f32[320,128]{1,0:T(8,128)S(1)} %constant_dynamic-slice_fusion.1), channel_id=1, source_target_pairs={{0,1},{1,0},{2,3},{3,2},{4,5},{5,4},{6,7},{7,6},{8,9},{9,8},{10,11... | collective-permute-start | bytes 491528 | tf_op jit(solution)/shard_map/ppermute | solution.py:48
  147.0 9.0 %collective-permute-start.9 = (f32[640,128]{1,0:T(8,128)S(1)}, f32[640,128]{1,0:T(8,128)S(1)}, u32[]{:S(2)}, u32[]{:S(2)}) collective-permute-start(f32[640,128]{1,0:T(8,128)S(1)} %add.256), channel_id=1, source_target_pairs={{16,0},{17,1},{18,2},{19,3},{20,4},{21,5},{22,6},{23,7},{24,8},{25... | collective-permute-start | bytes 983048 | tf_op jit(solution)/shard_map/ppermute | solution.py:69
  149.4 5.3 %collective-permute-start.13 = (f32[320,128]{1,0:T(8,128)S(1)}, f32[320,128]{1,0:T(8,128)S(1)}, u32[]{:S(2)}, u32[]{:S(2)}) collective-permute-start(f32[320,128]{1,0:T(8,128)S(1)} %get-tuple-element.34), channel_id=1, source_target_pairs={{0,1},{1,0},{2,3},{3,2},{4,5},{5,4},{6,7},{7,6},{8,9},{9,8},{10,11... | collective-permute-start | bytes 491528 | tf_op jit(solution)/shard_map/ppermute | solution.py:48
  172.0 1.2 collective-permute-start.16
  173.3 3.7 %collective-permute-start.17 = (f32[8,128]{1,0:T(8,128)S(1)}, f32[8,128]{1,0:T(8,128)S(1)}, u32[]{:S(2)}, u32[]{:S(2)}) collective-permute-start(f32[8,128]{1,0:T(8,128)S(1)} %add.288), channel_id=1, source_target_pairs={{0,4},{2,6},{4,0},{6,2},{8,12},{10,14},{12,8},{14,10},{1,5},{3,7},... | collective-permute-start | bytes 12296 | tf_op jit(solution)/shard_map/ppermute | solution.py:284
  177.0 4.5 %collective-permute-start.18 = (f32[8,128]{1,0:T(8,128)S(1)}, f32[8,128]{1,0:T(8,128)S(1)}, u32[]{:S(2)}, u32[]{:S(2)}) collective-permute-start(f32[8,128]{1,0:T(8,128)S(1)} %add.289), channel_id=1, source_target_pairs={{0,8},{2,10},{4,12},{6,14},{8,0},{10,2},{12,4},{14,6},{1,9},{3,11}... | collective-permute-start | bytes 12296 | tf_op jit(solution)/shard_map/ppermute | solution.py:284
  181.5 3.6 %collective-permute-start.19 = (f32[8,128]{1,0:T(8,128)S(1)}, f32[8,128]{1,0:T(8,128)S(1)}, u32[]{:S(2)}, u32[]{:S(2)}) collective-permute-start(f32[8,128]{1,0:T(8,128)S(1)} %add.290), channel_id=1, source_target_pairs={{0,1},{1,0},{2,3},{3,2},{4,5},{5,4},{6,7},{7,6},{8,9},{9,8},{10,11... | collective-permute-start | bytes 12296 | tf_op jit(solution)/shard_map/ppermute | solution.py:284
  185.1 3.6 %collective-permute-start.20 = (f32[8,128]{1,0:T(8,128)S(1)}, f32[8,128]{1,0:T(8,128)S(1)}, u32[]{:S(2)}, u32[]{:S(2)}) collective-permute-start(f32[8,128]{1,0:T(8,128)S(1)} %add.291), channel_id=1, source_target_pairs={{0,16},{16,0},{1,17},{17,1},{2,18},{18,2},{3,19},{19,3},{4,20},{20... | collective-permute-start | bytes 12296 | tf_op jit(solution)/shard_map/ppermute | solution.py:284
  185.7 11.8 %collective-permute-start.22 = (f32[640,128]{1,0:T(8,128)S(1)}, f32[640,128]{1,0:T(8,128)S(1)}, u32[]{:S(2)}, u32[]{:S(2)}) collective-permute-start(f32[640,128]{1,0:T(8,128)S(1)} %copy-done.6), channel_id=1, source_target_pairs={{16,0},{17,1},{18,2},{19,3},{20,4},{21,5},{22,6},{23,7},{24,8},{25... | collective-permute-start | bytes 983048 | tf_op jit(solution)/shard_map/ppermute | solution.py:69
  187.0 13.8 %collective-permute-start.21 = (f32[640,128]{1,0:T(8,128)S(1)}, f32[640,128]{1,0:T(8,128)}, u32[]{:S(2)}, u32[]{:S(2)}) collective-permute-start(f32[640,128]{1,0:T(8,128)S(1)} %copy-done.8), channel_id=1, source_target_pairs={{16,0},{17,1},{18,2},{19,3},{20,4},{21,5},{22,6},{23,7},{24,8},{25... | collective-permute-start | bytes 983048 | tf_op jit(solution)/shard_map/ppermute | solution.py:69
  (15 other events, 174.6 us)
where the time goes:
time: 205 us; the launch traced here: 203 us
  starting transfers between devices  52.7 us (26%)
  waiting for transfers between devices  49.5 us (24%)
  matrix products  43 us (21%)
  other arithmetic  24.4 us (12%)
  local copies, waits for them, and re-layouts  16.9 us (8%)
  between operations  16.8 us (8%)
    dot_general x19, matrix products, contract(): lax.dot_general(left, right, ((over[:1], over[1:]), ((), ())), precision=...  43 us
    ppermute x9, waiting for transfers between devices, rotated(): lax.ppermute(block, axis, [(i, (i + distance) % size) for i in range(size)])  28.4 us
    ppermute x8, starting transfers between devices, mixtures(): arrived[distance] = lax.ppermute(field, 'sub', route)  13.6 us
    ppermute x9, starting transfers between devices, rotated(): lax.ppermute(block, axis, [(i, (i + distance) % size) for i in range(size)])  11 us
    all_to_all x2, starting transfers between devices, covariance(): owned = lax.all_to_all(amplitudes, 'col', 0, 0, tiled=True)  9.58 us
    ppermute x5, waiting for transfers between devices, on_device(): sums = sums + lax.ppermute(sums, axis, [(i, i ^ step) for i in range(size)])  8.11 us
    all_to_all x2, starting transfers between devices, covariance(): returned = lax.all_to_all(back, 'col', 0, 0, tiled=True)  7.77 us
    ppermute x5, starting transfers between devices, on_device(): sums = sums + lax.ppermute(sums, axis, [(i, i ^ step) for i in range(size)])  5.92 us
  transfers between devices with their start and end apart: 27, of which 16 were waited for; matrix products, arithmetic and copies ran while one was open for 37% of the time, Pallas kernels for 0%

commit v1 on v0

v1 whole, which is shorter than its diff:
```python
import math

import jax
import jax.numpy as jnp
import numpy as np
from jax import lax
from jax.experimental import pallas as pl
from jax.experimental.pallas import tpu as pltpu
from jax.sharding import PartitionSpec as P

KW = 128


F32 = jnp.float32
BF16 = jnp.bfloat16


def spectrum(scales, limits, total, count):
    waves = jnp.arange(count, dtype=jnp.int32)
    wavef = waves.astype(jnp.float32)
    decay = jnp.exp(-0.5 * (2.0 * math.pi * wavef[None, :] * scales[:, None] / total) ** 2)
    factor = jnp.where(waves == 0, 1.0, 2.0).astype(jnp.float32) / total
    keep = (waves[None, :] < limits[:, None]).astype(jnp.float32)
    values = decay * factor[None, :] * keep
    return jnp.concatenate([values, values], axis=1)


def spectral_table(count, coarse, fine):
    total = coarse * fine

    def small(columns):
        phase = columns[:, None] * jnp.arange(count, dtype=jnp.int32)[None, :] % total
        angle = 2.0 * math.pi / total * phase.astype(F32)
        return jnp.cos(angle), jnp.sin(angle)

    cos_a, sin_a = (t[:, None, :] for t in small(jnp.arange(coarse, dtype=jnp.int32) * fine))
    cos_b, sin_b = (t[None, :, :] for t in small(jnp.arange(fine, dtype=jnp.int32)))
    table = jnp.concatenate([cos_a * cos_b - sin_a * sin_b, sin_a * cos_b + cos_a * sin_b], axis=2)
    return table.reshape(total, 2 * count)


def rotated(block, axis, distance):
    size = lax.axis_size(axis)
    return lax.ppermute(block, axis, [(i, (i + distance) % size) for i in range(size)])


def mixtures(field, plans):
    size = lax.axis_size("sub")
    here = lax.axis_index("sub")
    masked = []
    for matrix, unread, zero in plans:
        weights = np.array(matrix, dtype=np.float32)
        live = np.ones_like(weights, dtype=bool)
        live[list(unread), :] = False
        live[:, list(zero)] = False
        masked.append((weights, live))
    arrived = {0: field}
    cells = {0: [(i, i) for i in range(size)]}
    for distance in range(1, size):
        steps = [((source + distance) % size, source) for source in range(size)]
        cells[distance] = [c for c in steps if any(w[c] * l[c] for w, l in masked)]
        if cells[distance]:
            arrived[distance] = lax.ppermute(field, "sub", [(source, dest) for dest, source in cells[distance]])
    results = []
    for weights, live in masked:
        total = None
        for distance, block in arrived.items():
            used = {float(weights[c]) for c in cells[distance] if live[c]}
            if not used or used == {0.0}:
                continue
            if len(used) > 1:
                factors = np.zeros(size, np.float32)
                for dest, source in cells[distance]:
                    factors[dest] = weights[dest, source]
                block = block * jnp.asarray(factors)[here]
            elif used != {1.0}:
                block = block * used.pop()
            total = block if total is None else total + block
        results.append(total)
    return results


def plus(*terms):
    kept = [term for term in terms if term is not None]
    return sum(kept[1:], kept[0]) if kept else None


def halves(value):
    high = value.astype(BF16)
    return high, (value - high.astype(F32)).astype(BF16)


def contract(left, right, over):
    return lax.dot_general(left, right, (((over[0],), (over[1],)), ((), ())), preferred_element_type=F32)


def contract3(left, right, over):
    left_high, left_low = left
    right_high, right_low = right
    return (
        contract(left_high, right_low, over)
        + contract(left_low, right_high, over)
        + contract(left_high, right_high, over)
    )


def mixed_rows(left, right, fine, over):
    high, low = left
    right_high, right_low = right
    if high.shape[0] == fine:
        return contract3(left, right, over)
    wide = contract(jnp.concatenate([high, low], axis=0), right_high, over)
    exact = wide[:fine] + wide[high.shape[0] :] + contract(high[:fine], right_low, over)
    return jnp.concatenate([exact, wide[fine : high.shape[0]]], axis=0)


def fine_low(value, fine):
    high = value.astype(BF16)
    return high, (value[:fine] - high[:fine].astype(F32)).astype(BF16)


def call(kernel, out, inputs, flops, grid=None, in_specs=None, out_specs=None, scratch=()):
    vmem = pl.BlockSpec(memory_space=pltpu.VMEM)
    smem = pl.BlockSpec(memory_space=pltpu.SMEM)
    if in_specs is None:
        in_specs = [smem if jnp.issubdtype(x.dtype, jnp.integer) else vmem for x in inputs]
        out_specs = jax.tree.map(lambda _: vmem, out)
    size = sum(math.prod(x.shape) * x.dtype.itemsize for x in [*inputs, *jax.tree.leaves(out)])
    return pl.pallas_call(
        kernel,
        out_shape=out,
        grid=grid or (),
        in_specs=in_specs,
        out_specs=out_specs,
        scratch_shapes=scratch,
        cost_estimate=pl.CostEstimate(flops=flops, bytes_accessed=size, transcendentals=0),
        compiler_params=pltpu.CompilerParams(vmem_limit_bytes=40 * 1024 * 1024),
    )(*inputs)


def shape(*dims):
    return jax.ShapeDtypeStruct(dims, F32)


def on_device(
    first_rhs,
    innovations,
    start_mult,
    trajectory,
    weight_in,
    weight_out,
    vertical_modes,
    length_scale,
    band_limit,
    obs_col,
    obs_count,
    obs_var,
):
    data = innovations[0]
    variance = obs_var[0][:, None]
    depth, width = first_rhs.shape[1:]
    slots = data.shape[0]
    subs = lax.axis_size("sub")
    shards = lax.axis_size("col")
    groups = lax.axis_size("grp")
    here = lax.axis_index("sub")
    column_index = lax.axis_index("col")
    group_index = lax.axis_index("grp")
    total_cols = width * shards
    hidden = weight_in.shape[0]
    half_modes = vertical_modes.shape[0]
    owned_modes = half_modes // shards
    rows = width // groups
    steps = 4
    block = hidden // steps

    ones = np.ones((subs, subs))
    up = np.eye(subs, k=1)
    down = np.eye(subs, k=-1)
    later = np.triu(ones)
    earlier = np.tril(ones)
    first = (0,)
    place = jnp.stack([group_index, here]).astype(jnp.int32)

    def turned(place_ref, ref, value):
        for step in range(groups):
            ref[step] = value_rows(value, lax.rem(place_ref[0] + step, groups))

    def value_rows(value, index):
        total = value[:rows]
        for other in range(1, groups):
            total = jnp.where(index == other, value[other * rows : (other + 1) * rows], total)
        return total

    def own_rows(place_ref, ref):
        return ref[pl.ds(pl.multiple_of(place_ref[0] * rows, rows), rows), :]

    def own(field):
        return lax.dynamic_slice_in_dim(field, group_index * rows, rows, 0)

    def sent(partial):
        return [rotated(partial, "grp", step) for step in range(1, groups)]

    def sent_parts(parts):
        return [parts[0], *(rotated(parts[step], "grp", step) for step in range(1, groups))]

    def summed_own(parts):
        return plus(*sent_parts(parts))

    def summed(partial):
        return plus(partial, *sent(partial))

    def joined(part):
        whole = lax.dynamic_update_slice_in_dim(jnp.zeros((width, depth), F32), part, group_index * rows, 0)
        for step in range(1, groups):
            source = (group_index - step) % groups
            whole = lax.dynamic_update_slice_in_dim(whole, rotated(part, "grp", step), source * rows, 0)
        return whole

    before = lax.ppermute(trajectory[0].astype(F32), "sub", [(i, i + 1) for i in range(subs - 1)])

    local_cols = obs_col[0] - column_index * width
    live = (jnp.arange(slots, dtype=jnp.int32) < obs_count[0, 0]).astype(F32)
    pick = (jnp.arange(width, dtype=jnp.int32)[:, None] == local_cols[None, :]).astype(F32)
    mine = ((local_cols // rows) == group_index).astype(F32)[:, None]
    pick = pick * live[None, :]

    def picked(values, chosen):
        high, low = halves(values)
        chosen = chosen.astype(BF16)
        return contract(chosen, high, (1, 0)) + contract(chosen, low, (1, 0))

    def seen_by(chosen, field):
        high, low = halves(field)
        chosen = chosen.astype(BF16)
        return contract(chosen, high, (0, 0)) + contract(chosen, low, (0, 0))

    def opening(start_ref, rhs_ref, data_ref, variance_ref, pick_ref, modes_ref, start_out, push_out, rhs_out, amp_ref):
        start_t = start_ref[...].T
        push_t = picked(data_ref[...] / variance_ref[...], pick_ref[...])
        start_out[...] = start_t
        push_out[...] = push_t
        rhs_out[...] = rhs_ref[...].T
        modes = halves(modes_ref[...])
        amp_ref[:, :width] = contract(modes[0], start_t.astype(BF16), (1, 1))
        amp_ref[:, width:] = contract3(modes, halves(push_t), (1, 1))

    start, push, rhs, amp_early = call(
        opening,
        [shape(width, depth)] * 3 + [shape(half_modes, 2 * width)],
        [start_mult[0], first_rhs[0], data, variance, pick, vertical_modes],
        8 * half_modes * depth * width,
    )
    whole_spec = [pl.BlockSpec(memory_space=pltpu.SMEM)]

    def fixed(*dims):
        return pl.BlockSpec(dims, lambda i: (0,) * len(dims))

    in_block = pl.BlockSpec((block, depth), lambda i: (i, 0))
    out_block = pl.BlockSpec((depth, block), lambda i: (0, i))
    slope_block = pl.BlockSpec((width, block), lambda i: (0, i))

    def slopes_and_adjoint(place_ref, fine_ref, rough_ref, before_ref, win_ref, wout_ref, fine_out, rough_out, slopes_ref, total_ref, turned_ref):
        index = pl.program_id(0)

        @pl.when(index == 0)
        def _():
            total_ref[...] = jnp.zeros_like(total_ref)
            turned_ref[...] = before_ref[...].T.astype(BF16)

        win = halves(win_ref[...])
        wout = halves(wout_ref[...])
        state = turned_ref[...]
        bend = jnp.tanh(contract(state, win[1], (1, 1)) + contract(state, win[0], (1, 1)))
        slopes = (1.0 - bend * bend) * (place_ref[1] > 0).astype(F32)
        slopes_ref[...] = slopes
        fields = fine_low(jnp.concatenate([fine_ref[...], rough_ref[...]], axis=0), width)
        inner = mixed_rows(fields, wout, width, (1, 0)) * jnp.concatenate([slopes, slopes], axis=0)
        total_ref[...] += mixed_rows(fine_low(inner, width), win, width, (1, 0))

        @pl.when(index == steps - 1)
        def _():
            fine_out[...] = total_ref[:width]
            turned(place_ref, rough_out, total_ref[width:])

    push_fed, push_later = mixtures(push, [(later, first, ()), (later, (), ())])
    pull0_part, pull2_parts, slopes = call(
        slopes_and_adjoint,
        [shape(width, depth), shape(groups, rows, depth), shape(width, hidden)],
        [place, start, push_fed, before, weight_in, weight_out],
        20 * hidden * depth * width,
        grid=(steps,),
        in_specs=whole_spec + [fixed(width, depth)] * 2 + [fixed(depth, width), in_block, out_block],
        out_specs=[fixed(width, depth), fixed(groups, rows, depth), slope_block],
        scratch=[pltpu.VMEM((2 * width, depth), F32), pltpu.VMEM((width, depth), BF16)],
    )

    def adjoint(field):
        def kernel(field_ref, slopes_ref, win_ref, wout_ref, total_ref):
            @pl.when(pl.program_id(0) == 0)
            def _():
                total_ref[...] = jnp.zeros_like(total_ref)

            inner = contract3(halves(field_ref[...]), halves(wout_ref[...]), (1, 0)) * slopes_ref[...]
            total_ref[...] += contract3(halves(inner), halves(win_ref[...]), (1, 0))

        return call(
            kernel,
            shape(width, depth),
            [field, slopes, weight_in, weight_out],
            12 * hidden * depth * width,
            grid=(steps,),
            in_specs=[fixed(width, depth), slope_block, in_block, out_block],
            out_specs=fixed(width, depth),
        )

    def tangent(fine, rough=None):
        count = 1 if rough is None else 2

        def kernel(place_ref, *refs):
            fields, (slopes_ref, win_ref, wout_ref), outs, total_ref = (
                refs[:count],
                refs[count : count + 3],
                refs[count + 3 : -1],
                refs[-1],
            )

            @pl.when(pl.program_id(0) == 0)
            def _():
                total_ref[...] = jnp.zeros_like(total_ref)

            both = fine_low(jnp.concatenate([r[...] for r in fields], axis=0), width)
            slope = slopes_ref[...]
            inner = mixed_rows(both, halves(win_ref[...]), width, (1, 1)) * jnp.concatenate([slope] * count, axis=0)
            total_ref[...] += mixed_rows(fine_low(inner, width), halves(wout_ref[...]), width, (1, 1))

            @pl.when(pl.program_id(0) == steps - 1)
            def _():
                for i, out in enumerate(outs):
                    turned(place_ref, out, total_ref[i * width : (i + 1) * width])

        return call(
            kernel,
            [shape(groups, rows, depth)] * count,
            [place, fine, *([] if rough is None else [rough]), slopes, weight_in, weight_out],
            (12 if rough is None else 16) * hidden * depth * width,
            grid=(steps,),
            in_specs=whole_spec + [fixed(width, depth)] * count + [slope_block, in_block, out_block],
            out_specs=[fixed(groups, rows, depth)] * count,
            scratch=[pltpu.VMEM((count * width, depth), F32)],
        )

    seed, pull0_part = lax.optimization_barrier((jnp.zeros((), jnp.int32), pull0_part))
    first_mode = group_index * half_modes + column_index * owned_modes + seed
    owned_scales = lax.dynamic_slice_in_dim(length_scale, first_mode, owned_modes, 0)
    owned_limits = lax.dynamic_slice_in_dim(band_limit, first_mode, owned_modes, 0)
    owned_spec = spectrum(owned_scales, owned_limits, total_cols, KW)
    fine_cols = 1 << (total_cols.bit_length() // 2)
    table = spectral_table(KW, total_cols // fine_cols, fine_cols)

    def amplitudes(field_parts):
        def kernel(*refs):
            modes_ref, whole_ref, amp_ref = refs[-3:]
            whole = plus(*(r[...] for r in refs[:-3]))
            whole_ref[...] = whole
            amp_ref[...] = contract3(halves(modes_ref[...]), halves(whole), (1, 1))

        return call(
            kernel,
            [shape(width, depth), shape(half_modes, width)],
            [*field_parts, vertical_modes],
            6 * half_modes * depth * width,
        )

    def correlated(amp):
        count = amp.shape[1] // width
        owned = lax.all_to_all(amp.reshape(shards, owned_modes, count * width), "col", 0, 0, tiled=True)

        def kernel(owned_ref, table_ref, spec_ref, back_ref):
            parts = halves(table_ref[...])
            for i in range(count):
                lanes = slice(i * width, (i + 1) * width)
                modes = jnp.concatenate([owned_ref[c][:, lanes] for c in range(shards)], axis=1)
                coeffs = contract3(halves(modes), parts, (1, 0)) * spec_ref[...]
                back = contract3(halves(coeffs), parts, (1, 1))
                for c in range(shards):
                    back_ref[c, :, lanes] = back[:, c * width : (c + 1) * width]

        back = call(
            kernel,
            shape(*owned.shape),
            [owned, table, owned_spec],
            12 * owned_modes * count * total_cols * 2 * KW,
        )
        returned = lax.all_to_all(back, "col", 0, 0, tiled=True)
        return returned.reshape(half_modes, count * width)

    def back_to_columns(returned):
        def kernel(returned_ref, modes_ref, out_ref):
            out_ref[...] = contract3(halves(returned_ref[...].T), halves(modes_ref[...]), (1, 0))

        return call(
            kernel, shape(width, depth), [returned, vertical_modes], 6 * half_modes * depth * width
        )

    def back_to_columns_early(returned):
        def kernel(place_ref, returned_ref, modes_ref, rough_out, fine_out):
            modes = halves(modes_ref[...])
            back = returned_ref[...].T
            turned(place_ref, rough_out, contract(back[:width].astype(BF16), modes[0], (1, 0)))
            fine_out[...] = contract3(halves(back[width:]), modes, (1, 0))

        return call(
            kernel,
            [shape(groups, rows, depth), shape(width, depth)],
            [place, returned, vertical_modes],
            8 * half_modes * depth * width,
        )

    def covariance_sum(field):
        return summed(back_to_columns(correlated(amplitudes([field])[1])))

    pull0, amp_pull = amplitudes([pull0_part, *sent(pull0_part)])
    cov_start_parts, cov_push_part = back_to_columns_early(correlated(amp_early))
    cov_push = summed(cov_push_part)
    push_feed, push_state = mixtures(
        cov_push, [(down @ earlier @ later, first, ()), (earlier @ later, (), ())]
    )
    rhs_feed, rhs_state = mixtures(rhs, [(down @ earlier, first, ()), (earlier, (), ())])
    fed_rhs_parts, fed_push_parts = tangent(rhs_feed, push_feed)
    fed_rhs = summed_own(fed_rhs_parts)
    fed_push = summed_own(fed_push_parts)
    cov_start = summed_own(cov_start_parts)
    pull2 = summed_own(pull2_parts)

    cov_pull = summed(back_to_columns(correlated(amp_pull)))
    pull_feed, pull_state = mixtures(
        cov_pull, [(down @ earlier @ later @ up, first, first), (earlier @ later @ up, (), first)]
    )
    fed_pull = summed_own(tangent(pull_feed)[0])
    pull0_fed, pull0_later = mixtures(pull0, [(later @ up, first, first), (later @ up, (), first)])

    moved = fed_rhs - fed_pull
    moved_turn = fed_pull + fed_push
    turn_mult = plus(pull0_later, push_later)
    pull1 = None
    if pull0_fed is not None:
        pull1 = summed(adjoint(pull0_fed))
        pull1_fed, pull1_later = mixtures(pull1, [(later @ up, first, first), (later @ up, (), first)])
        pull2 = pull2 + own(summed(adjoint(pull0_fed - pull1_fed)))
        turn_mult = turn_mult - pull1_later
        cov_pull1 = covariance_sum(pull1)
        pull1_feed, pull1_state = mixtures(
            cov_pull1, [(down @ earlier @ later @ up, first, first), (earlier @ later @ up, (), first)]
        )
        push_state = push_state - pull1_state
        moved_turn = moved_turn - summed_own(tangent(pull1_feed)[0])
    moved_feed, moved_state = mixtures(moved, [(down @ earlier, first, first), (earlier, (), first)])
    if moved_feed is not None:
        moved_turn = moved_turn + summed_own(tangent(joined(moved_feed))[0])

    (start_next,) = mixtures(own(start), [(up, (), ())])
    pull_shift = 2.0 * own(pull0)
    pull_step = own(pull0) - pull2
    if pull1 is not None:
        own_pull1 = own(pull1)
        pull_shift = pull_shift - own_pull1
        pull_step = pull_step - own_pull1
        (pull_next,) = mixtures(own(pull0), [(up, (), first)])
    (shift_next,) = mixtures(pull_shift, [(up, (), first)])
    (step_next,) = mixtures(pull_step, [(up, (), first)])
    if pull1 is None:
        pull_next = 0.5 * shift_next

    def inner_products(
        place_ref, rhs_ref, cov_start_ref, moved_ref, moved_turn_ref, moved_state_ref, data_ref, variance_ref,
        pick_ref, mine_ref, rhs_state_ref, pull_state_ref, push_state_ref, start_ref, push_ref,
        start_next_ref, pull_next_ref, shift_next_ref, step_next_ref, sums_ref,
    ):
        moved = moved_ref[...]
        pull_own = own_rows(place_ref, pull_state_ref)
        state = own_rows(place_ref, rhs_state_ref) - pull_own
        turn_state = moved_state_ref[...] + pull_own + own_rows(place_ref, push_state_ref)
        res1 = own_rows(place_ref, rhs_ref) - cov_start_ref[...]
        image1 = res1 - moved
        turn1 = image1 - moved + moved_turn_ref[...]
        mine = mine_ref[...]
        chosen = own_rows(place_ref, pick_ref)
        res2 = data_ref[...] * mine
        seen = seen_by(chosen, state)
        image2 = res2 + seen
        turn2 = image2 + seen - seen_by(chosen, turn_state)
        push = own_rows(place_ref, push_ref)
        from_next = start_next_ref[...] - own_rows(place_ref, start_ref)
        res3 = from_next + pull_next_ref[...]
        image3 = from_next + shift_next_ref[...] + push
        turn3 = image3 + step_next_ref[...] + push + picked(seen / variance_ref[...], chosen)
        res = (res1, res2, res3)
        image = (image1, image2, image3)
        turn = (turn1, turn2, turn3)
        lane = lax.broadcasted_iota(jnp.int32, sums_ref.shape, 1)
        sums = jnp.zeros(sums_ref.shape, F32)
        for i, (left, right) in enumerate(((image, res), (image, image), (turn, res), (turn, image), (turn, turn))):
            value = sum(jnp.sum(a * b) for a, b in zip(left, right))
            sums = jnp.where(lane == i, value, sums)
        sums_ref[...] = sums

    everyone = ("sub", "col", "grp")
    devices = subs * shards * groups
    sums = call(
        inner_products,
        shape(devices, 128),
        [
            place, rhs, cov_start, moved, moved_turn, moved_state, data, variance, pick, mine,
            rhs_state, pull_state, push_state, start, push, start_next, pull_next, shift_next, step_next,
        ],
        1000000,
    )
    sums = lax.all_to_all(sums, everyone, 0, 0, tiled=True)
    moved_state = joined(moved_state)

    def closing(
        sums_ref, start_ref, pull_later_ref, turn_mult_ref, data_ref, variance_ref, pick_ref,
        rhs_state_ref, pull_state_ref, push_state_ref, moved_state_ref, mult_ref, obs_ref, inc_ref,
    ):
        totals = jnp.sum(sums_ref[...], axis=0, keepdims=True)
        upper, square, turn_res, turn_image, turn_square = (totals[:, i : i + 1] for i in range(5))
        alpha = upper / square
        alpha_next = (upper - alpha * square - alpha * (turn_res - alpha * turn_image)) / (
            square - 2.0 * alpha * turn_image + alpha * alpha * turn_square
        )
        keep = alpha + alpha_next * (1.0 - alpha)
        mixed = alpha * alpha_next
        start_t = start_ref[...]
        state = rhs_state_ref[...] - pull_state_ref[...]
        turn_state = moved_state_ref[...] + pull_state_ref[...] + push_state_ref[...]
        mult_ref[...] = (start_t + keep * (pull_later_ref[...] - start_t) - mixed * turn_mult_ref[...]).T
        inc_ref[...] = (keep * state + mixed * turn_state).T
        seen = seen_by(pick_ref[...], state)
        data_t = data_ref[...]
        obs_ref[...] = ((alpha + alpha_next) * data_t - mixed * (data_t + seen)) / variance_ref[...]

    multiplier, obs_multiplier, increment = call(
        closing,
        [shape(depth, width), shape(slots, depth), shape(depth, width)],
        [
            sums, start, pull0_later, turn_mult, data, variance, pick,
            rhs_state, pull_state, push_state, moved_state,
        ],
        1000000,
    )
    return (multiplier[None], obs_multiplier[None], increment[None])


def solution(mesh):
    placed = (
        P("sub", None, "col"),
        P("sub", "col", None),
        P("sub", None, "col"),
        P("sub", None, "col"),
        P("grp", None),
        P(None, "grp"),
        P("grp", None),
        P(),
        P(),
        P("sub", "col"),
        P("sub", "col"),
        P("sub", "col"),
    )
    return jax.shard_map(
        on_device,
        mesh=mesh,
        in_specs=placed,
        out_specs=(P("sub", None, "col"), P("sub", "col", None), P("sub", None, "col")),
        check_vma=False,
    )
```

time: 205 us -> 172 us (0.84)
  matrix products: 43 us -> 0 us
  Pallas kernels: 0 us -> 36.5 us
  between operations: 16.8 us -> 1.74 us
  other arithmetic: 24.4 us -> 9.73 us
  local copies, waits for them, and re-layouts: 16.9 us -> 24.2 us
  waiting for transfers between devices: 49.5 us -> 42.3 us
  starting transfers between devices: 52.7 us -> 55.8 us
    dot_general x19 -> x0, matrix products: 43 us -> none  [contract(): lax.dot_general(left, right, ((over[:1], over[1:]), ((), ())), precision=...]
    pallas_call x0 -> x11, Pallas kernels: none -> 36.5 us  [call(): pl.pallas_call(kernel, out_shape=out, grid=grid or (), in_specs=in_specs,...]
    unnamed x40 -> x42, local copies, waits for them, and re-layouts: 2.37 us -> 17.6 us
    ppermute x9, waiting for transfers between devices: 28.4 us -> 19.5 us  [rotated(): lax.ppermute(block, axis, [(i, (i + distance) % size) for i in range(size)])]
    all_to_all x4 -> x5, starting transfers between devices: 17.4 us -> 24.6 us  [the longest x2 10.7 us: correlated(): lax.all_to_all(amp.reshape(shards, owned_modes, count * width), 'col', 0,...]
    cos x2 -> x1, other arithmetic: 5.32 us -> 0.15 us  [small(): return (jnp.cos(angle), jnp.sin(angle))]
    broadcast_in_dim x3 -> x0, other arithmetic: 4.86 us -> none  [on_device(): return (multiplier[None], obs_multiplier[None], increment[None])]
    ppermute x14 -> x9, starting transfers between devices: 24.4 us -> 21.2 us  [the longest x8 17.8 us: mixtures(): lax.ppermute(field, 'sub', [(source, dest) for dest, source in cells[dist...]
  transfers between devices with their start and end apart: 27 -> 23, of which waited for: 16 -> 11; matrix products, arithmetic and copies ran while one was open for 37% -> 9% of each run, Pallas kernels for 0% -> 19%
where the time goes in v1:
time: 172 us; the launch traced here: 170 us
  starting transfers between devices  55.8 us (32%)
  waiting for transfers between devices  42.3 us (25%)
  Pallas kernels  36.5 us (21%)
  local copies, waits for them, and re-layouts  24.2 us (14%)
  other arithmetic  9.73 us (6%)
  between operations  1.74 us (1%)
    pallas_call x11, Pallas kernels, call(): pl.pallas_call(kernel, out_shape=out, grid=grid or (), in_specs=in_specs,...  36.5 us
    ppermute x9, waiting for transfers between devices, rotated(): lax.ppermute(block, axis, [(i, (i + distance) % size) for i in range(size)])  19.5 us
    ppermute x8, starting transfers between devices, mixtures(): lax.ppermute(field, 'sub', [(source, dest) for dest, source in cells[dist...  17.8 us
    unnamed x42, local copies, waits for them, and re-layouts  17.6 us
    all_to_all x2, starting transfers between devices, correlated(): lax.all_to_all(amp.reshape(shards, owned_modes, count * width), 'col', 0,...  10.7 us
    ppermute x9, starting transfers between devices, rotated(): lax.ppermute(block, axis, [(i, (i + distance) % size) for i in range(size)])  9.94 us
    all_to_all x2, starting transfers between devices, correlated(): returned = lax.all_to_all(back, 'col', 0, 0, tiled=True)  9.2 us
    ppermute x1, waiting for transfers between devices, on_device(): lax.ppermute(trajectory[0].astype(F32), 'sub', [(i, i + 1) for i in range...  7.24 us
  transfers between devices with their start and end apart: 23, of which 11 were waited for; matrix products, arithmetic and copies ran while one was open for 9% of the time, Pallas kernels for 19%

profile of v1, /device:TPU:0, one launch (start us, length us, event | category | flops | bytes accessed | tf_op | source)
XLA Modules:
  0.0 170.2 jit_solution(3015918570841269003)
XLA Ops:
  9.0 6.4 %all-to-all-start = ((f32[8,40,256]{2,1,0:T(8,128)}), f32[8,40,256]{2,1,0:T(8,128)}, u32[]{:S(2)}, u32[]{:S(2)}) async-start(f32[8,40,256]{2,1,0:T(8,128)} %bitcast.8), calls=%async_computation | async-start | bytes 655360 | tf_op jit(solution)/shard_map/all_to_all | solution.py:377
  16.3 3.4 %collective-permute-start = (f32[640,128]{1,0:T(8,128)S(1)}, f32[640,128]{1,0:T(8,128)S(1)}, u32[]{:S(2)}, u32[]{:S(2)}) collective-permute-start(f32[640,128]{1,0:T(8,128)S(1)} %bitcast_convert_fusion), channel_id=1, source_target_pairs={{0,16},{1,17},{2,18},{3,19},{4,20},{5,21},{6,22},{7,23},{8,24},{9,... | collective-permute-start | bytes 983048 | tf_op jit(solution)/shard_map/ppermute | solution.py:220
  20.1 7.2 %collective-permute-done.before_ref = f32[640,128]{1,0:T(8,128)S(1)} collective-permute-done((f32[640,128]{1,0:T(8,128)S(1)}, f32[640,128]{1,0:T(8,128)S(1)}, u32[]{:S(2)}, u32[]{:S(2)}) %collective-permute-start) | collective-permute-done | bytes 327712 | tf_op jit(solution)/shard_map/ppermute | solution.py:220
  27.3 2.5 %copy-done = f32[2048,640]{1,0:T(8,128)S(1)} copy-done((f32[2048,640]{1,0:T(8,128)S(1)}, f32[2048,640]{1,0:T(8,128)}, u32[]{:S(2)}) %copy-start) | copy-done | bytes 5242904
  29.8 2.5 %copy-done.2 = f32[640,2048]{1,0:T(8,128)S(1)} copy-done((f32[640,2048]{1,0:T(8,128)S(1)}, f32[640,2048]{1,0:T(8,128)}, u32[]{:S(2)}) %copy-start.2) | copy-done | bytes 5242904
  32.3 7.9 %shard_map.149 = (f32[128,640]{1,0:T(8,128)}, f32[2,64,640]{2,1,0:T(8,128)S(1)}, f32[128,2048]{1,0:T(8,128)S(1)}) custom-call(s32[2]{0:T(128)S(1)} %pad_add_fusion.place_ref, f32[128,640]{1,0:T(8,128)S(1)} %get-tuple-element.23.fine_ref.start_ref, f32[128,640]{1,0:T(8,128)S(1)} %get-tuple-element.24.rough_ref.push_ref, ...), custom_call_target="tpu_custom_call" | custom-call | flops 3355443200 | bytes 13172744 | tf_op jit(solution)/shard_map/pallas_call | solution.py:129
  43.4 6.3 %collective-permute-done.6.refs_1_ = f32[128,640]{1,0:T(8,128)} collective-permute-done((f32[128,640]{1,0:T(8,128)}, f32[128,640]{1,0:T(8,128)}, u32[]{:S(2)}, u32[]{:S(2)}) %collective-permute-start.6) | collective-permute-done | bytes 327712 | tf_op jit(solution)/shard_map/ppermute | solution.py:44
  52.7 4.3 %all-to-all-start.2 = ((f32[8,40,128]{2,1,0:T(8,128)}), f32[8,40,128]{2,1,0:T(8,128)S(1)}, u32[]{:S(2)}, u32[]{:S(2)}) async-start(f32[8,40,128]{2,1,0:T(8,128)} %bitcast.69), calls=%async_computation.2 | async-start | bytes 327680 | tf_op jit(solution)/shard_map/all_to_all | solution.py:377
  57.1 2.8 %shard_map.150 = f32[8,40,256]{2,1,0:T(8,128)S(1)} custom-call(f32[8,40,256]{2,1,0:T(8,128)} %all-to-all-done.owned_ref, f32[1024,256]{1,0:T(8,128)S(1)} %pad_maximum_fusion.table_ref, f32[40,256]{1,0:T(8,128)S(1)} %pad_maximum_fusion.1.spec_ref), custom_call_target="tpu_custom_call" | custom-call | flops 251658240 | bytes 1744896 | tf_op jit(solution)/shard_map/pallas_call | solution.py:129
  60.7 3.5 %all-to-all-done.2.owned_ref = f32[8,40,128]{2,1,0:T(8,128)S(1)} async-done(((f32[8,40,128]{2,1,0:T(8,128)}), f32[8,40,128]{2,1,0:T(8,128)S(1)}, u32[]{:S(2)}, u32[]{:S(2)}) %all-to-all-start.2) | async-done | bytes 163872 | tf_op jit(solution)/shard_map/all_to_all | solution.py:377
  64.2 4.1 %all-to-all-start.1 = ((f32[8,40,256]{2,1,0:T(8,128)}), f32[8,40,256]{2,1,0:T(8,128)}, u32[]{:S(2)}, u32[]{:S(2)}) async-start(f32[8,40,256]{2,1,0:T(8,128)} %copy-done.9), calls=%async_computation.1 | async-start | bytes 655360 | tf_op jit(solution)/shard_map/all_to_all | solution.py:395
  68.3 1.6 slice_bitcast_fusion.2
  72.7 6.0 %collective-permute-start.2 = (f32[128,640]{1,0:T(8,128)}, f32[128,640]{1,0:T(8,128)}, u32[]{:S(2)}, u32[]{:S(2)}) collective-permute-start(f32[128,640]{1,0:T(8,128)} %copy-done.12), channel_id=1, source_target_pairs={{0,16},{1,17},{2,18},{3,19},{4,20},{5,21},{6,22},{7,23},{8,24},{9,... | collective-permute-start | bytes 983048 | tf_op jit(solution)/shard_map/ppermute | solution.py:63
  82.6 1.9 %shard_map.154 = f32[8,40,128]{2,1,0:T(8,128)} custom-call(f32[8,40,128]{2,1,0:T(8,128)S(1)} %all-to-all-done.2.owned_ref, f32[1024,256]{1,0:T(8,128)S(1)} %pad_maximum_fusion.table_ref, f32[40,256]{1,0:T(8,128)S(1)} %pad_maximum_fusion.1.spec_ref), custom_call_target="tpu_custom_call" | custom-call | flops 125829120 | bytes 1417216 | tf_op jit(solution)/shard_map/pallas_call | solution.py:129
  84.5 5.1 %all-to-all-start.3 = ((f32[8,40,128]{2,1,0:T(8,128)}), f32[8,40,128]{2,1,0:T(8,128)S(1)}, u32[]{:S(2)}, u32[]{:S(2)}) async-start(f32[8,40,128]{2,1,0:T(8,128)} %shard_map.154), calls=%async_computation.3 | async-start | bytes 327680 | tf_op jit(solution)/shard_map/all_to_all | solution.py:395
  89.7 1.8 %fusion.1 = (f32[64,640]{1,0:T(8,128)}, f32[64,640]{1,0:T(8,128)S(1)}) fusion(f32[64,640]{1,0:T(8,128)} %collective-permute-done.13, f32[2,64,640]{2,1,0:T(8,128)} %copy-done.16, f32[128,640]{1,0:T(8,128)} %copy-done.20, s32[]{:T(128)S(6)} %select_n.77), kind=kLoop, calls=%fused_computation.10 | loop fusion | flops 122880 | bytes 819204 | tf_op jit(solution)/shard_map/sub | solution.py:464
  95.9 2.3 %shard_map.151 = (f32[2,64,640]{2,1,0:T(8,128)S(1)}, f32[128,640]{1,0:T(8,128)}) custom-call(s32[2]{0:T(128)S(1)} %pad_add_fusion.place_ref, f32[320,256]{1,0:T(8,128)} %bitcast.12.returned_ref, f32[320,640]{1,0:T(8,128)S(1)} %copy-done.5), custom_call_target="tpu_custom_call" | custom-call | flops 209715200 | bytes 1802248 | tf_op jit(solution)/shard_map/pallas_call | solution.py:129
  103.5 1.9 %add_add_fusion.turn_mult_ref = f32[128,640]{1,0:T(8,128)} fusion(f32[128,640]{1,0:T(8,128)} %collective-permute-done.15.pull_later_ref, f32[128,640]{1,0:T(8,128)S(1)} %copy-done.11, f32[128,640]{1,0:T(8,128)} %collective-permute-done.16), kind=kLoop, calls=%fused_computation.3 | loop fusion | flops 163840 | bytes 1310720 | tf_op jit(solution)/shard_map/add | solution.py:85
  105.3 4.6 %collective-permute-done.3 = f32[128,640]{1,0:T(8,128)} collective-permute-done((f32[128,640]{1,0:T(8,128)}, f32[128,640]{1,0:T(8,128)}, u32[]{:S(2)}, u32[]{:S(2)}) %collective-permute-start.3) | collective-permute-done | bytes 327712 | tf_op jit(solution)/shard_map/ppermute | solution.py:44
  111.0 4.1 %collective-permute-start.4 = (f32[128,640]{1,0:T(8,128)S(1)}, f32[128,640]{1,0:T(8,128)S(1)}, u32[]{:S(2)}, u32[]{:S(2)}) collective-permute-start(f32[128,640]{1,0:T(8,128)S(1)} %add.120), channel_id=1, source_target_pairs={{0,16},{16,0},{1,17},{17,1},{2,18},{18,2},{3,19},{19,3},{4,20},{20... | collective-permute-start | bytes 983048 | tf_op jit(solution)/shard_map/ppermute | solution.py:63
  116.4 2.5 %copy-done.1 = f32[2048,640]{1,0:T(8,128)S(1)} copy-done((f32[2048,640]{1,0:T(8,128)S(1)}, f32[2048,640]{1,0:T(8,128)}, u32[]{:S(2)}) %copy-start.1) | copy-done | bytes 5242904
  118.9 2.5 %copy-done.3 = f32[640,2048]{1,0:T(8,128)S(1)} copy-done((f32[640,2048]{1,0:T(8,128)S(1)}, f32[640,2048]{1,0:T(8,128)}, u32[]{:S(2)}) %copy-start.3) | copy-done | bytes 5242904
  121.3 6.8 %shard_map.156 = f32[2,64,640]{2,1,0:T(8,128)S(1)} custom-call(s32[2]{0:T(128)S(1)} %pad_add_fusion.place_ref, f32[128,640]{1,0:T(8,128)S(1)} %add.123.refs_0_, f32[128,2048]{1,0:T(8,128)S(1)} %get-tuple-element.29.refs_2_.refs_1_, f32[2048,640]{1,0:T(8,128)S(1)} %copy-done.1, f32[640,2048]{1,0:T(8,128)S(1)} %copy-done.3), custom_call_target="tpu_custom_call" | custom-call | flops 2013265920 | bytes 12189704 | tf_op jit(solution)/shard_map/pallas_call | solution.py:129
  129.5 6.6 %shard_map.152 = (f32[2,64,640]{2,1,0:T(8,128)S(1)}, f32[2,64,640]{2,1,0:T(8,128)S(1)}) custom-call(s32[2]{0:T(128)S(1)} %pad_add_fusion.place_ref, f32[128,640]{1,0:T(8,128)} %collective-permute-done.2.refs_0_, f32[128,640]{1,0:T(8,128)S(1)} %get-tuple-element.42.refs_1_, f32[128,2048]{1,0:T(8,128)S(1)} %get-tuple-element.29.refs_2_.refs_1_, ...), custom_call_target="tpu_custom_call" | custom-call | flops 2684354560 | bytes 12845064 | tf_op jit(solution)/shard_map/pallas_call | solution.py:129
  139.9 3.4 %collective-permute-done.5 = f32[64,640]{1,0:T(8,128)S(1)} collective-permute-done((f32[64,640]{1,0:T(8,128)S(1)}, f32[64,640]{1,0:T(8,128)S(1)}, u32[]{:S(2)}, u32[]{:S(2)}) %collective-permute-start.5) | collective-permute-done | bytes 163872 | tf_op jit(solution)/shard_map/ppermute | solution.py:44
  144.5 2.2 %collective-permute-done.9 = f32[64,640]{1,0:T(8,128)S(1)} collective-permute-done((f32[64,640]{1,0:T(8,128)S(1)}, f32[64,640]{1,0:T(8,128)S(1)}, u32[]{:S(2)}, u32[]{:S(2)}) %collective-permute-start.9) | collective-permute-done | bytes 163872 | tf_op jit(solution)/shard_map/ppermute | solution.py:44
  148.5 1.8 %collective-permute-done.1 = f32[64,640]{1,0:T(8,128)S(1)} collective-permute-done((f32[64,640]{1,0:T(8,128)S(1)}, f32[64,640]{1,0:T(8,128)S(1)}, u32[]{:S(2)}, u32[]{:S(2)}) %collective-permute-start.1) | collective-permute-done | bytes 163872 | tf_op jit(solution)/shard_map/ppermute | solution.py:44
  150.3 3.3 %collective-permute-done.10 = f32[128,640]{1,0:T(8,128)S(1)} collective-permute-done((f32[128,640]{1,0:T(8,128)S(1)}, f32[128,640]{1,0:T(8,128)S(1)}, u32[]{:S(2)}, u32[]{:S(2)}) %collective-permute-start.10) | collective-permute-done | bytes 327712 | tf_op jit(solution)/shard_map/ppermute | solution.py:63
  153.7 2.2 %shard_map.157 = f32[32,128]{1,0:T(8,128)} custom-call(s32[2]{0:T(128)S(1)} %pad_add_fusion.place_ref, f32[128,640]{1,0:T(8,128)S(1)} %copy-done.13, f32[64,640]{1,0:T(8,128)S(1)} %bitcast_add_fusion.3.cov_start_ref, f32[64,640]{1,0:T(8,128)S(1)} %get-tuple-element.40.moved_ref.moved_state_ref, f32[64,640]{1,0:T(8,128)S(1)} %get-tuple-element.43.moved_turn_ref, ...), custom_call_target="tpu_custom_call" | custom-call | flops 1000000 | bytes 3490312 | tf_op jit(solution)/shard_map/pallas_call | solution.py:129
  155.9 4.7 %all-to-all-start.4 = ((f32[32,1,128]{2,1,0:T(1,128)}), f32[32,1,128]{2,1,0:T(1,128)S(1)}, u32[]{:S(2)}, u32[]{:S(2)}) async-start(f32[32,1,128]{2,1,0:T(1,128)} %bitcast.28), calls=%async_computation.4 | async-start | bytes 32768 | tf_op jit(solution)/shard_map/all_to_all | solution.py:519
  160.7 7.1 %all-to-all-done.4 = f32[32,1,128]{2,1,0:T(1,128)S(1)} async-done(((f32[32,1,128]{2,1,0:T(1,128)}), f32[32,1,128]{2,1,0:T(1,128)S(1)}, u32[]{:S(2)}, u32[]{:S(2)}) %all-to-all-start.4) | async-done | bytes 16416 | tf_op jit(solution)/shard_map/all_to_all | solution.py:519
  167.8 2.4 %shard_map.158 = (f32[640,128]{1,0:T(8,128)}, f32[64,640]{1,0:T(8,128)}, f32[640,128]{1,0:T(8,128)}) custom-call(f32[32,128]{1,0:T(8,128)S(1)} %bitcast.70, f32[128,640]{1,0:T(8,128)S(1)} %get-tuple-element.23.fine_ref.start_ref, f32[128,640]{1,0:T(8,128)} %collective-permute-done.15.pull_later_ref, f32[128,640]{1,0:T(8,128)S(1)} %copy-done.8, ...), custom_call_target="tpu_custom_call" | custom-call | flops 1000000 | bytes 3326208 | tf_op jit(solution)/shard_map/pallas_call | solution.py:129
  (104 shorter events, 42.8 us)
Async XLA Ops:
  9.0 31.2 %copy-start.10 = (f32[128,640]{1,0:T(8,128)}, f32[128,640]{1,0:T(8,128)S(1)}, u32[]{:S(2)}) copy-start(f32[128,640]{1,0:T(8,128)S(1)} %get-tuple-element.24.rough_ref.push_ref) | copy-start | bytes 983044
  9.0 43.7 %all-to-all-start = ((f32[8,40,256]{2,1,0:T(8,128)}), f32[8,40,256]{2,1,0:T(8,128)}, u32[]{:S(2)}, u32[]{:S(2)}) async-start(f32[8,40,256]{2,1,0:T(8,128)} %bitcast.8), calls=%async_computation | async-start | bytes 655360 | tf_op jit(solution)/shard_map/all_to_all | solution.py:377
  16.3 11.0 %collective-permute-start = (f32[640,128]{1,0:T(8,128)S(1)}, f32[640,128]{1,0:T(8,128)S(1)}, u32[]{:S(2)}, u32[]{:S(2)}) collective-permute-start(f32[640,128]{1,0:T(8,128)S(1)} %bitcast_convert_fusion), channel_id=1, source_target_pairs={{0,16},{1,17},{2,18},{3,19},{4,20},{5,21},{6,22},{7,23},{8,24},{9,... | collective-permute-start | bytes 983048 | tf_op jit(solution)/shard_map/ppermute | solution.py:220
  27.3 2.5 %copy-start = (f32[2048,640]{1,0:T(8,128)S(1)}, f32[2048,640]{1,0:T(8,128)}, u32[]{:S(2)}) copy-start(f32[2048,640]{1,0:T(8,128)} %refs_2_.3) | copy-start | bytes 15728644
  32.3 17.4 %copy-start.5 = (f32[320,640]{1,0:T(8,128)S(1)}, f32[320,640]{1,0:T(8,128)}, u32[]{:S(2)}) copy-start(f32[320,640]{1,0:T(8,128)} %modes_ref.5) | copy-start | bytes 2457604
  40.1 9.6 %collective-permute-start.6 = (f32[128,640]{1,0:T(8,128)}, f32[128,640]{1,0:T(8,128)}, u32[]{:S(2)}, u32[]{:S(2)}) collective-permute-start(f32[128,640]{1,0:T(8,128)} %get-tuple-element.31.refs_0_), channel_id=1, source_target_pairs={{0,1},{1,0},{2,3},{3,2},{4,5},{5,4},{6,7},{7,6},{8,9},{9,8},{10,11... | collective-permute-start | bytes 983048 | tf_op jit(solution)/shard_map/ppermute | solution.py:44
  52.7 11.5 %all-to-all-start.2 = ((f32[8,40,128]{2,1,0:T(8,128)}), f32[8,40,128]{2,1,0:T(8,128)S(1)}, u32[]{:S(2)}, u32[]{:S(2)}) async-start(f32[8,40,128]{2,1,0:T(8,128)} %bitcast.69), calls=%async_computation.2 | async-start | bytes 327680 | tf_op jit(solution)/shard_map/all_to_all | solution.py:377
  64.2 20.3 %all-to-all-start.1 = ((f32[8,40,256]{2,1,0:T(8,128)}), f32[8,40,256]{2,1,0:T(8,128)}, u32[]{:S(2)}, u32[]{:S(2)}) async-start(f32[8,40,256]{2,1,0:T(8,128)} %copy-done.9), calls=%async_computation.1 | async-start | bytes 655360 | tf_op jit(solution)/shard_map/all_to_all | solution.py:395
  69.9 19.8 %collective-permute-start.13 = (f32[64,640]{1,0:T(8,128)}, f32[64,640]{1,0:T(8,128)}, u32[]{:S(2)}, u32[]{:S(2)}) collective-permute-start(f32[64,640]{1,0:T(8,128)} %slice_bitcast_fusion.2), channel_id=1, source_target_pairs={{0,1},{1,0},{2,3},{3,2},{4,5},{5,4},{6,7},{7,6},{8,9},{9,8},{10,11... | collective-permute-start | bytes 491528 | tf_op jit(solution)/shard_map/ppermute | solution.py:44
  71.4 30.7 %collective-permute-start.16 = (f32[128,640]{1,0:T(8,128)}, f32[128,640]{1,0:T(8,128)}, u32[]{:S(2)}, u32[]{:S(2)}) collective-permute-start(f32[128,640]{1,0:T(8,128)} %copy-done.10), channel_id=1, source_target_pairs={{16,0},{17,1},{18,2},{19,3},{20,4},{21,5},{22,6},{23,7},{24,8},{25... | collective-permute-start | bytes 983048 | tf_op jit(solution)/shard_map/ppermute | solution.py:63
  72.7 22.1 %collective-permute-start.2 = (f32[128,640]{1,0:T(8,128)}, f32[128,640]{1,0:T(8,128)}, u32[]{:S(2)}, u32[]{:S(2)}) collective-permute-start(f32[128,640]{1,0:T(8,128)} %copy-done.12), channel_id=1, source_target_pairs={{0,16},{1,17},{2,18},{3,19},{4,20},{5,21},{6,22},{7,23},{8,24},{9,... | collective-permute-start | bytes 983048 | tf_op jit(solution)/shard_map/ppermute | solution.py:63
  79.4 74.3 %collective-permute-start.11 = (f32[64,640]{1,0:T(8,128)}, f32[64,640]{1,0:T(8,128)}, u32[]{:S(2)}, u32[]{:S(2)}) collective-permute-start(f32[64,640]{1,0:T(8,128)} %constant_dynamic-slice_fusion), channel_id=1, source_target_pairs={{16,0},{17,1},{18,2},{19,3},{20,4},{21,5},{22,6},{23,7},{24,8},{25... | collective-permute-start | bytes 491528 | tf_op jit(solution)/shard_map/ppermute | solution.py:63
  81.4 22.1 %collective-permute-start.15 = (f32[128,640]{1,0:T(8,128)}, f32[128,640]{1,0:T(8,128)}, u32[]{:S(2)}, u32[]{:S(2)}) collective-permute-start(f32[128,640]{1,0:T(8,128)} %copy-done.20), channel_id=1, source_target_pairs={{16,0},{17,1},{18,2},{19,3},{20,4},{21,5},{22,6},{23,7},{24,8},{25... | collective-permute-start | bytes 983048 | tf_op jit(solution)/shard_map/ppermute | solution.py:63
  84.5 18.9 %copy-start.11 = (f32[128,640]{1,0:T(8,128)S(1)}, f32[128,640]{1,0:T(8,128)}, u32[]{:S(2)}) copy-start(f32[128,640]{1,0:T(8,128)} %copy-done.10) | copy-start | bytes 983044
  84.5 15.0 %all-to-all-start.3 = ((f32[8,40,128]{2,1,0:T(8,128)}), f32[8,40,128]{2,1,0:T(8,128)S(1)}, u32[]{:S(2)}, u32[]{:S(2)}) async-start(f32[8,40,128]{2,1,0:T(8,128)} %shard_map.154), calls=%async_computation.3 | async-start | bytes 327680 | tf_op jit(solution)/shard_map/all_to_all | solution.py:395
  91.4 10.2 %collective-permute-start.12 = (f32[64,640]{1,0:T(8,128)S(1)}, f32[64,640]{1,0:T(8,128)S(1)}, u32[]{:S(2)}, u32[]{:S(2)}) collective-permute-start(f32[64,640]{1,0:T(8,128)S(1)} %get-tuple-element.45), channel_id=1, source_target_pairs={{16,0},{17,1},{18,2},{19,3},{20,4},{21,5},{22,6},{23,7},{24,8},{25... | collective-permute-start | bytes 491528 | tf_op jit(solution)/shard_map/ppermute | solution.py:63
  99.0 10.9 %collective-permute-start.3 = (f32[128,640]{1,0:T(8,128)}, f32[128,640]{1,0:T(8,128)}, u32[]{:S(2)}, u32[]{:S(2)}) collective-permute-start(f32[128,640]{1,0:T(8,128)} %get-tuple-element.28), channel_id=1, source_target_pairs={{0,1},{1,0},{2,3},{3,2},{4,5},{5,4},{6,7},{7,6},{8,9},{9,8},{10,11... | collective-permute-start | bytes 983048 | tf_op jit(solution)/shard_map/ppermute | solution.py:44
  101.6 14.7 %collective-permute-start.7 = (f32[128,640]{1,0:T(8,128)S(1)}, f32[128,640]{1,0:T(8,128)S(1)}, u32[]{:S(2)}, u32[]{:S(2)}) collective-permute-start(f32[128,640]{1,0:T(8,128)S(1)} %shard_map.155), channel_id=1, source_target_pairs={{0,1},{1,0},{2,3},{3,2},{4,5},{5,4},{6,7},{7,6},{8,9},{9,8},{10,11... | collective-permute-start | bytes 983048 | tf_op jit(solution)/shard_map/ppermute | solution.py:44
  102.1 51.5 %collective-permute-start.14 = (f32[64,640]{1,0:T(8,128)}, f32[64,640]{1,0:T(8,128)S(1)}, u32[]{:S(2)}, u32[]{:S(2)}) collective-permute-start(f32[64,640]{1,0:T(8,128)} %get-tuple-element.44), channel_id=1, source_target_pairs={{16,0},{17,1},{18,2},{19,3},{20,4},{21,5},{22,6},{23,7},{24,8},{25... | collective-permute-start | bytes 491528 | tf_op jit(solution)/shard_map/ppermute | solution.py:63
  111.0 17.8 %collective-permute-start.4 = (f32[128,640]{1,0:T(8,128)S(1)}, f32[128,640]{1,0:T(8,128)S(1)}, u32[]{:S(2)}, u32[]{:S(2)}) collective-permute-start(f32[128,640]{1,0:T(8,128)S(1)} %add.120), channel_id=1, source_target_pairs={{0,16},{16,0},{1,17},{17,1},{2,18},{18,2},{3,19},{19,3},{4,20},{20... | collective-permute-start | bytes 983048 | tf_op jit(solution)/shard_map/ppermute | solution.py:63
  116.4 2.5 %copy-start.1 = (f32[2048,640]{1,0:T(8,128)S(1)}, f32[2048,640]{1,0:T(8,128)}, u32[]{:S(2)}) copy-start(f32[2048,640]{1,0:T(8,128)} %refs_2_.3) | copy-start | bytes 15728644
  128.2 10.1 %collective-permute-start.8 = (f32[64,640]{1,0:T(8,128)S(1)}, f32[64,640]{1,0:T(8,128)S(1)}, u32[]{:S(2)}, u32[]{:S(2)}) collective-permute-start(f32[64,640]{1,0:T(8,128)S(1)} %slice_bitcast_fusion), channel_id=1, source_target_pairs={{0,1},{1,0},{2,3},{3,2},{4,5},{5,4},{6,7},{7,6},{8,9},{9,8},{10,11... | collective-permute-start | bytes 491528 | tf_op jit(solution)/shard_map/ppermute | solution.py:44
  129.4 8.9 %copy-start.15 = (f32[2,64,640]{2,1,0:T(8,128)S(1)}, f32[2,64,640]{2,1,0:T(8,128)}, u32[]{:S(2)}) copy-start(f32[2,64,640]{2,1,0:T(8,128)} %copy-done.14) | copy-start | bytes 983044
  129.4 24.2 %copy-start.7 = (f32[1,64,640]{2,1,0:T(8,128)S(1)}, f32[1,64,640]{2,1,0:T(8,128)}, u32[]{:S(2)}) copy-start(f32[1,64,640]{2,1,0:T(8,128)} %param.14) | copy-start | bytes 491524
  129.5 24.2 %copy-start.13 = (f32[128,640]{1,0:T(8,128)S(1)}, f32[128,640]{1,0:T(8,128)}, u32[]{:S(2)}) copy-start(f32[128,640]{1,0:T(8,128)} %copy-done.12) | copy-start | bytes 983044
  136.1 31.7 %copy-start.8 = (f32[128,640]{1,0:T(8,128)S(1)}, f32[128,640]{1,0:T(8,128)}, u32[]{:S(2)}) copy-start(f32[128,640]{1,0:T(8,128)} %add_add_fusion.turn_mult_ref) | copy-start | bytes 983044
  136.1 7.1 %collective-permute-start.5 = (f32[64,640]{1,0:T(8,128)S(1)}, f32[64,640]{1,0:T(8,128)S(1)}, u32[]{:S(2)}, u32[]{:S(2)}) collective-permute-start(f32[64,640]{1,0:T(8,128)S(1)} %slice_bitcast_fusion.4), channel_id=1, source_target_pairs={{0,1},{1,0},{2,3},{3,2},{4,5},{5,4},{6,7},{7,6},{8,9},{9,8},{10,11... | collective-permute-start | bytes 491528 | tf_op jit(solution)/shard_map/ppermute | solution.py:44
  137.7 9.1 %collective-permute-start.9 = (f32[64,640]{1,0:T(8,128)S(1)}, f32[64,640]{1,0:T(8,128)S(1)}, u32[]{:S(2)}, u32[]{:S(2)}) collective-permute-start(f32[64,640]{1,0:T(8,128)S(1)} %slice_bitcast_fusion.3), channel_id=1, source_target_pairs={{0,1},{1,0},{2,3},{3,2},{4,5},{5,4},{6,7},{7,6},{8,9},{9,8},{10,11... | collective-permute-start | bytes 491528 | tf_op jit(solution)/shard_map/ppermute | solution.py:44
  138.3 12.0 %collective-permute-start.1 = (f32[64,640]{1,0:T(8,128)S(1)}, f32[64,640]{1,0:T(8,128)S(1)}, u32[]{:S(2)}, u32[]{:S(2)}) collective-permute-start(f32[64,640]{1,0:T(8,128)S(1)} %slice_bitcast_fusion.5), channel_id=1, source_target_pairs={{0,1},{1,0},{2,3},{3,2},{4,5},{5,4},{6,7},{7,6},{8,9},{9,8},{10,11... | collective-permute-start | bytes 491528 | tf_op jit(solution)/shard_map/ppermute | solution.py:44
  143.3 10.4 %collective-permute-start.10 = (f32[128,640]{1,0:T(8,128)S(1)}, f32[128,640]{1,0:T(8,128)S(1)}, u32[]{:S(2)}, u32[]{:S(2)}) collective-permute-start(f32[128,640]{1,0:T(8,128)S(1)} %add.123.refs_0_), channel_id=1, source_target_pairs={{16,0},{17,1},{18,2},{19,3},{20,4},{21,5},{22,6},{23,7},{24,8},{25... | collective-permute-start | bytes 983048 | tf_op jit(solution)/shard_map/ppermute | solution.py:63
  146.9 13.8 %collective-permute-start.17 = (f32[64,640]{1,0:T(8,128)S(1)}, f32[64,640]{1,0:T(8,128)S(1)}, u32[]{:S(2)}, u32[]{:S(2)}) collective-permute-start(f32[64,640]{1,0:T(8,128)S(1)} %get-tuple-element.40.moved_ref.moved_state_ref), channel_id=1, source_target_pairs={{0,1},{1,0},{2,3},{3,2},{4,5},{5,4},{6,7},{7,6},{8,9},{9,8},{10,11... | collective-permute-start | bytes 491528 | tf_op jit(solution)/shard_map/ppermute | solution.py:44
  155.9 11.9 %all-to-all-start.4 = ((f32[32,1,128]{2,1,0:T(1,128)}), f32[32,1,128]{2,1,0:T(1,128)S(1)}, u32[]{:S(2)}, u32[]{:S(2)}) async-start(f32[32,1,128]{2,1,0:T(1,128)} %bitcast.28), calls=%async_computation.4 | async-start | bytes 32768 | tf_op jit(solution)/shard_map/all_to_all | solution.py:519
  (12 other events, 14.3 us)

commit v2 on v1

--- a/solution.py
+++ b/solution.py
@@ -25,11 +25,11 @@
     return jnp.concatenate([values, values], axis=1)
 
 
-def spectral_table(count, coarse, fine):
+def spectral_table(count, coarse, fine, origin):
     total = coarse * fine
 
     def small(columns):
-        phase = columns[:, None] * jnp.arange(count, dtype=jnp.int32)[None, :] % total
+        phase = (columns[:, None] + origin) * jnp.arange(count, dtype=jnp.int32)[None, :] % total
         angle = 2.0 * math.pi / total * phase.astype(F32)
         return jnp.cos(angle), jnp.sin(angle)
 
@@ -119,7 +119,7 @@
     return high, (value[:fine] - high[:fine].astype(F32)).astype(BF16)
 
 
-def call(kernel, out, inputs, flops, grid=None, in_specs=None, out_specs=None, scratch=()):
+def call(kernel, out, inputs, flops, vmem_mib=16, grid=None, in_specs=None, out_specs=None, scratch=()):
     vmem = pl.BlockSpec(memory_space=pltpu.VMEM)
     smem = pl.BlockSpec(memory_space=pltpu.SMEM)
     if in_specs is None:
@@ -134,7 +134,7 @@
         out_specs=out_specs,
         scratch_shapes=scratch,
         cost_estimate=pl.CostEstimate(flops=flops, bytes_accessed=size, transcendentals=0),
-        compiler_params=pltpu.CompilerParams(vmem_limit_bytes=40 * 1024 * 1024),
+        compiler_params=pltpu.CompilerParams(vmem_limit_bytes=vmem_mib * 1024 * 1024),
     )(*inputs)
 
 
@@ -201,11 +201,8 @@
     def sent(partial):
         return [rotated(partial, "grp", step) for step in range(1, groups)]
 
-    def sent_parts(parts):
-        return [parts[0], *(rotated(parts[step], "grp", step) for step in range(1, groups))]
-
     def summed_own(parts):
-        return plus(*sent_parts(parts))
+        return plus(parts[0], *(rotated(parts[step], "grp", step) for step in range(1, groups)))
 
     def summed(partial):
         return plus(partial, *sent(partial))
@@ -289,6 +286,7 @@
         [shape(width, depth), shape(groups, rows, depth), shape(width, hidden)],
         [place, start, push_fed, before, weight_in, weight_out],
         20 * hidden * depth * width,
+        vmem_mib=20,
         grid=(steps,),
         in_specs=whole_spec + [fixed(width, depth)] * 2 + [fixed(depth, width), in_block, out_block],
         out_specs=[fixed(width, depth), fixed(groups, rows, depth), slope_block],
@@ -309,6 +307,7 @@
             shape(width, depth),
             [field, slopes, weight_in, weight_out],
             12 * hidden * depth * width,
+            vmem_mib=20,
             grid=(steps,),
             in_specs=[fixed(width, depth), slope_block, in_block, out_block],
             out_specs=fixed(width, depth),
@@ -318,12 +317,7 @@
         count = 1 if rough is None else 2
 
         def kernel(place_ref, *refs):
-            fields, (slopes_ref, win_ref, wout_ref), outs, total_ref = (
-                refs[:count],
-                refs[count : count + 3],
-                refs[count + 3 : -1],
-                refs[-1],
-            )
+            fields, (slopes_ref, win_ref, wout_ref, out_ref, total_ref) = refs[:count], refs[count:]
 
             @pl.when(pl.program_id(0) == 0)
             def _():
@@ -336,27 +330,34 @@
 
             @pl.when(pl.program_id(0) == steps - 1)
             def _():
-                for i, out in enumerate(outs):
-                    turned(place_ref, out, total_ref[i * width : (i + 1) * width])
-
-        return call(
+                for i in range(count):
+                    turned(
+                        place_ref,
+                        out_ref.at[:, i * rows : (i + 1) * rows],
+                        total_ref[i * width : (i + 1) * width],
+                    )
+
+        parts = call(
             kernel,
-            [shape(groups, rows, depth)] * count,
+            shape(groups, count * rows, depth),
             [place, fine, *([] if rough is None else [rough]), slopes, weight_in, weight_out],
             (12 if rough is None else 16) * hidden * depth * width,
+            vmem_mib=20,
             grid=(steps,),
             in_specs=whole_spec + [fixed(width, depth)] * count + [slope_block, in_block, out_block],
-            out_specs=[fixed(groups, rows, depth)] * count,
+            out_specs=fixed(groups, count * rows, depth),
             scratch=[pltpu.VMEM((count * width, depth), F32)],
         )
-
-    seed, pull0_part = lax.optimization_barrier((jnp.zeros((), jnp.int32), pull0_part))
+        return summed_own(parts)
+
+    seed, amp_early = lax.optimization_barrier((place[0], amp_early))
+    seed = seed - group_index
     first_mode = group_index * half_modes + column_index * owned_modes + seed
     owned_scales = lax.dynamic_slice_in_dim(length_scale, first_mode, owned_modes, 0)
     owned_limits = lax.dynamic_slice_in_dim(band_limit, first_mode, owned_modes, 0)
     owned_spec = spectrum(owned_scales, owned_limits, total_cols, KW)
     fine_cols = 1 << (total_cols.bit_length() // 2)
-    table = spectral_table(KW, total_cols // fine_cols, fine_cols)
+    table = spectral_table(KW, total_cols // fine_cols, fine_cols, seed)
 
     def amplitudes(field_parts):
         def kernel(*refs):
@@ -387,10 +388,7 @@
                     back_ref[c, :, lanes] = back[:, c * width : (c + 1) * width]
 
         back = call(
-            kernel,
-            shape(*owned.shape),
-            [owned, table, owned_spec],
-            12 * owned_modes * count * total_cols * 2 * KW,
+            kernel, shape(*owned.shape), [owned, table, owned_spec], 12 * owned_modes * count * total_cols * 2 * KW
         )
         returned = lax.all_to_all(back, "col", 0, 0, tiled=True)
         return returned.reshape(half_modes, count * width)
@@ -399,54 +397,54 @@
         def kernel(returned_ref, modes_ref, out_ref):
             out_ref[...] = contract3(halves(returned_ref[...].T), halves(modes_ref[...]), (1, 0))
 
-        return call(
-            kernel, shape(width, depth), [returned, vertical_modes], 6 * half_modes * depth * width
-        )
-
-    def back_to_columns_early(returned):
-        def kernel(place_ref, returned_ref, modes_ref, rough_out, fine_out):
+        return call(kernel, shape(width, depth), [returned, vertical_modes], 6 * half_modes * depth * width)
+
+    def back_to_columns_early(returned, beside):
+        def kernel(place_ref, returned_ref, modes_ref, beside_ref, rough_out, fine_out):
             modes = halves(modes_ref[...])
             back = returned_ref[...].T
-            turned(place_ref, rough_out, contract(back[:width].astype(BF16), modes[0], (1, 0)))
+            turned(place_ref, rough_out.at[:, :rows], contract(back[:width].astype(BF16), modes[0], (1, 0)))
+            rough_out[:, rows:] = beside_ref[...]
             fine_out[...] = contract3(halves(back[width:]), modes, (1, 0))
 
         return call(
             kernel,
-            [shape(groups, rows, depth), shape(width, depth)],
-            [place, returned, vertical_modes],
+            [shape(groups, 2 * rows, depth), shape(width, depth)],
+            [place, returned, vertical_modes, beside],
             8 * half_modes * depth * width,
         )
 
     def covariance_sum(field):
-        return summed(back_to_columns(correlated(amplitudes([field])[1])))
+        amp = amplitudes([field])[1]
+        return summed(back_to_columns(correlated(amp)))
 
     pull0, amp_pull = amplitudes([pull0_part, *sent(pull0_part)])
-    cov_start_parts, cov_push_part = back_to_columns_early(correlated(amp_early))
+    beside_parts, cov_push_part = back_to_columns_early(correlated(amp_early), pull2_parts)
     cov_push = summed(cov_push_part)
-    push_feed, push_state = mixtures(
-        cov_push, [(down @ earlier @ later, first, ()), (earlier @ later, (), ())]
-    )
+    push_feed, push_state = mixtures(cov_push, [(down @ earlier @ later, first, ()), (earlier @ later, (), ())])
     rhs_feed, rhs_state = mixtures(rhs, [(down @ earlier, first, ()), (earlier, (), ())])
-    fed_rhs_parts, fed_push_parts = tangent(rhs_feed, push_feed)
-    fed_rhs = summed_own(fed_rhs_parts)
-    fed_push = summed_own(fed_push_parts)
-    cov_start = summed_own(cov_start_parts)
-    pull2 = summed_own(pull2_parts)
+    fed = tangent(rhs_feed, push_feed)
+    beside = summed_own(beside_parts)
+    cov_start, pull2 = beside[:rows], beside[rows:]
 
     cov_pull = summed(back_to_columns(correlated(amp_pull)))
     pull_feed, pull_state = mixtures(
         cov_pull, [(down @ earlier @ later @ up, first, first), (earlier @ later @ up, (), first)]
     )
-    fed_pull = summed_own(tangent(pull_feed)[0])
-    pull0_fed, pull0_later = mixtures(pull0, [(later @ up, first, first), (later @ up, (), first)])
-
-    moved = fed_rhs - fed_pull
-    moved_turn = fed_pull + fed_push
+    fed_pull = tangent(pull_feed)
+    pull0_fed, pull0_later, pull_next = mixtures(
+        pull0, [(later @ up, first, first), (later @ up, (), first), (up, (), first)]
+    )
+
+    moved = fed[:rows] - fed_pull
+    moved_turn = fed_pull + fed[rows:]
     turn_mult = plus(pull0_later, push_later)
     pull1 = None
     if pull0_fed is not None:
         pull1 = summed(adjoint(pull0_fed))
-        pull1_fed, pull1_later = mixtures(pull1, [(later @ up, first, first), (later @ up, (), first)])
+        pull1_fed, pull1_later, pull1_next = mixtures(
+            pull1, [(later @ up, first, first), (later @ up, (), first), (up, (), first)]
+        )
         pull2 = pull2 + own(summed(adjoint(pull0_fed - pull1_fed)))
         turn_mult = turn_mult - pull1_later
         cov_pull1 = covariance_sum(pull1)
@@ -454,29 +452,18 @@
             cov_pull1, [(down @ earlier @ later @ up, first, first), (earlier @ later @ up, (), first)]
         )
         push_state = push_state - pull1_state
-        moved_turn = moved_turn - summed_own(tangent(pull1_feed)[0])
+        moved_turn = moved_turn - tangent(pull1_feed)
     moved_feed, moved_state = mixtures(moved, [(down @ earlier, first, first), (earlier, (), first)])
     if moved_feed is not None:
-        moved_turn = moved_turn + summed_own(tangent(joined(moved_feed))[0])
-
-    (start_next,) = mixtures(own(start), [(up, (), ())])
-    pull_shift = 2.0 * own(pull0)
-    pull_step = own(pull0) - pull2
-    if pull1 is not None:
-        own_pull1 = own(pull1)
-        pull_shift = pull_shift - own_pull1
-        pull_step = pull_step - own_pull1
-        (pull_next,) = mixtures(own(pull0), [(up, (), first)])
-    (shift_next,) = mixtures(pull_shift, [(up, (), first)])
-    (step_next,) = mixtures(pull_step, [(up, (), first)])
-    if pull1 is None:
-        pull_next = 0.5 * shift_next
+        moved_turn = moved_turn + tangent(joined(moved_feed))
+    (next_pair,) = mixtures(jnp.concatenate([own(start), pull2], axis=0), [(up, (), ())])
 
     def inner_products(
         place_ref, rhs_ref, cov_start_ref, moved_ref, moved_turn_ref, moved_state_ref, data_ref, variance_ref,
         pick_ref, mine_ref, rhs_state_ref, pull_state_ref, push_state_ref, start_ref, push_ref,
-        start_next_ref, pull_next_ref, shift_next_ref, step_next_ref, sums_ref,
+        next_ref, pull_next_ref, *rest,
     ):
+        sums_ref = rest[-1]
         moved = moved_ref[...]
         pull_own = own_rows(place_ref, pull_state_ref)
         state = own_rows(place_ref, rhs_state_ref) - pull_own
@@ -491,10 +478,13 @@
         image2 = res2 + seen
         turn2 = image2 + seen - seen_by(chosen, turn_state)
         push = own_rows(place_ref, push_ref)
-        from_next = start_next_ref[...] - own_rows(place_ref, start_ref)
-        res3 = from_next + pull_next_ref[...]
-        image3 = from_next + shift_next_ref[...] + push
-        turn3 = image3 + step_next_ref[...] + push + picked(seen / variance_ref[...], chosen)
+        from_next = next_ref[:rows] - own_rows(place_ref, start_ref)
+        res3 = from_next + own_rows(place_ref, pull_next_ref)
+        step_next = own_rows(place_ref, pull_next_ref)
+        for pull1_next_ref in rest[:-1]:
+            step_next = step_next - own_rows(place_ref, pull1_next_ref)
+        image3 = res3 + step_next + push
+        turn3 = image3 + step_next - next_ref[rows:] + push + picked(seen / variance_ref[...], chosen)
         res = (res1, res2, res3)
         image = (image1, image2, image3)
         turn = (turn1, turn2, turn3)
@@ -512,7 +502,8 @@
         shape(devices, 128),
         [
             place, rhs, cov_start, moved, moved_turn, moved_state, data, variance, pick, mine,
-            rhs_state, pull_state, push_state, start, push, start_next, pull_next, shift_next, step_next,
+            rhs_state, pull_state, push_state, start, push, next_pair, pull_next,
+            *([] if pull1 is None else [pull1_next]),
         ],
         1000000,
     )

time: 172 us -> 161 us (0.936)
  starting transfers between devices: 55.8 us -> 48.3 us
  Pallas kernels: 36.5 us -> 31.6 us
    ppermute x8 -> x6, starting transfers between devices: 17.8 us -> 12.2 us  [mixtures(): lax.ppermute(field, 'sub', [(source, dest) for dest, source in cells[dist...]
    pallas_call x11, Pallas kernels: 36.5 us -> 31.6 us  [call(): pl.pallas_call(kernel, out_shape=out, grid=grid or (), in_specs=in_specs,...]
    ppermute x9 -> x7, waiting for transfers between devices: 19.5 us -> 23.4 us  [rotated(): lax.ppermute(block, axis, [(i, (i + distance) % size) for i in range(size)])]
    sub x1 -> x0, other arithmetic: 1.77 us -> none  [on_device(): pull_step = own(pull0) - pull2]
    unnamed x42 -> x44, local copies, waits for them, and re-layouts: 17.6 us -> 18.8 us
    ppermute x8 -> x6, waiting for transfers between devices: 4.89 us -> 3.88 us  [mixtures(): lax.ppermute(field, 'sub', [(source, dest) for dest, source in cells[dist...]
    ppermute x9 -> x7, starting transfers between devices: 9.94 us -> 8.95 us  [rotated(): lax.ppermute(block, axis, [(i, (i + distance) % size) for i in range(size)])]
  transfers between devices with their start and end apart: 23 -> 19, of which waited for: 11 -> 8; matrix products, arithmetic and copies ran while one was open for 9% -> 10% of each run, Pallas kernels for 19% -> 18%
where the time goes in v2:
time: 161 us; the launch traced here: 160 us
  starting transfers between devices  48.3 us (30%)
  waiting for transfers between devices  41.4 us (26%)
  Pallas kernels  31.6 us (20%)
  local copies, waits for them, and re-layouts  25.4 us (16%)
  other arithmetic  11.2 us (7%)
  between operations  1.73 us (1%)
    pallas_call x11, Pallas kernels, call(): pl.pallas_call(kernel, out_shape=out, grid=grid or (), in_specs=in_specs,...  31.6 us
    ppermute x7, waiting for transfers between devices, rotated(): lax.ppermute(block, axis, [(i, (i + distance) % size) for i in range(size)])  23.4 us
    unnamed x44, local copies, waits for them, and re-layouts  18.8 us
    ppermute x6, starting transfers between devices, mixtures(): lax.ppermute(field, 'sub', [(source, dest) for dest, source in cells[dist...  12.2 us
    all_to_all x2, starting transfers between devices, correlated(): lax.all_to_all(amp.reshape(shards, owned_modes, count * width), 'col', 0,...  10.7 us
    all_to_all x2, starting transfers between devices, correlated(): returned = lax.all_to_all(back, 'col', 0, 0, tiled=True)  9.04 us
    ppermute x7, starting transfers between devices, rotated(): lax.ppermute(block, axis, [(i, (i + distance) % size) for i in range(size)])  8.95 us
    all_to_all x1, waiting for transfers between devices, on_device(): sums = lax.all_to_all(sums, everyone, 0, 0, tiled=True)  6.21 us
  transfers between devices with their start and end apart: 19, of which 8 were waited for; matrix products, arithmetic and copies ran while one was open for 10% of the time, Pallas kernels for 18%

profile of v2, /device:TPU:0, one launch (start us, length us, event | category | flops | bytes accessed | tf_op | source)
XLA Modules:
  0.0 159.8 jit_solution(10363043814183690927)
XLA Ops:
  6.7 1.5 shard_map.148
  9.0 6.4 %all-to-all-start = ((f32[8,40,256]{2,1,0:T(8,128)}), f32[8,40,256]{2,1,0:T(8,128)S(1)}, u32[]{:S(2)}, u32[]{:S(2)}) async-start(f32[8,40,256]{2,1,0:T(8,128)} %bitcast.8), calls=%async_computation | async-start | bytes 655360 | tf_op jit(solution)/shard_map/all_to_all | solution.py:378
  16.3 3.4 %collective-permute-start = (f32[640,128]{1,0:T(8,128)S(1)}, f32[640,128]{1,0:T(8,128)S(1)}, u32[]{:S(2)}, u32[]{:S(2)}) collective-permute-start(f32[640,128]{1,0:T(8,128)S(1)} %bitcast_convert_fusion), channel_id=1, source_target_pairs={{0,16},{1,17},{2,18},{3,19},{4,20},{5,21},{6,22},{7,23},{8,24},{9,... | collective-permute-start | bytes 983048 | tf_op jit(solution)/shard_map/ppermute | solution.py:217
  21.6 5.7 %collective-permute-done.before_ref = f32[640,128]{1,0:T(8,128)S(1)} collective-permute-done((f32[640,128]{1,0:T(8,128)S(1)}, f32[640,128]{1,0:T(8,128)S(1)}, u32[]{:S(2)}, u32[]{:S(2)}) %collective-permute-start) | collective-permute-done | bytes 327712 | tf_op jit(solution)/shard_map/ppermute | solution.py:217
  27.3 2.5 %copy-done = f32[2048,640]{1,0:T(8,128)S(1)} copy-done((f32[2048,640]{1,0:T(8,128)S(1)}, f32[2048,640]{1,0:T(8,128)}, u32[]{:S(2)}) %copy-start) | copy-done | bytes 5242904
  29.8 2.5 %copy-done.2 = f32[640,2048]{1,0:T(8,128)S(1)} copy-done((f32[640,2048]{1,0:T(8,128)S(1)}, f32[640,2048]{1,0:T(8,128)}, u32[]{:S(2)}) %copy-start.2) | copy-done | bytes 5242904
  32.3 7.2 %shard_map.150 = (f32[128,640]{1,0:T(8,128)S(1)}, f32[2,64,640]{2,1,0:T(8,128)S(1)}, f32[128,2048]{1,0:T(8,128)S(1)}) custom-call(s32[2]{0:T(128)S(1)} %pad_add_fusion.place_ref, f32[128,640]{1,0:T(8,128)S(1)} %get-tuple-element.23.fine_ref.start_ref, f32[128,640]{1,0:T(8,128)S(1)} %get-tuple-element.24.rough_ref.push_ref, ...), custom_call_target="tpu_custom_call" | custom-call | flops 3355443200 | bytes 13172744 | tf_op jit(solution)/shard_map/pallas_call | solution.py:129
  39.5 1.6 collective-permute-start.6
  42.2 6.6 %collective-permute-done.6.refs_1_ = f32[128,640]{1,0:T(8,128)S(1)} collective-permute-done((f32[128,640]{1,0:T(8,128)S(1)}, f32[128,640]{1,0:T(8,128)S(1)}, u32[]{:S(2)}, u32[]{:S(2)}) %collective-permute-start.6) | collective-permute-done | bytes 327712 | tf_op jit(solution)/shard_map/ppermute | solution.py:44
  50.7 4.3 %all-to-all-start.2 = ((f32[8,40,128]{2,1,0:T(8,128)}), f32[8,40,128]{2,1,0:T(8,128)S(1)}, u32[]{:S(2)}, u32[]{:S(2)}) async-start(f32[8,40,128]{2,1,0:T(8,128)} %bitcast.17), calls=%async_computation.2 | async-start | bytes 327680 | tf_op jit(solution)/shard_map/all_to_all | solution.py:378
  57.4 1.8 %shard_map.149 = f32[8,40,256]{2,1,0:T(8,128)S(1)} custom-call(f32[8,40,256]{2,1,0:T(8,128)S(1)} %copy-done.9, f32[1024,256]{1,0:T(8,128)S(1)} %pad_maximum_fusion.table_ref, f32[40,256]{1,0:T(8,128)S(1)} %pad_maximum_fusion.2.spec_ref), custom_call_target="tpu_custom_call" | custom-call | flops 251658240 | bytes 1744896 | tf_op jit(solution)/shard_map/pallas_call | solution.py:129
  60.0 2.3 %all-to-all-done.2.owned_ref = f32[8,40,128]{2,1,0:T(8,128)S(1)} async-done(((f32[8,40,128]{2,1,0:T(8,128)}), f32[8,40,128]{2,1,0:T(8,128)S(1)}, u32[]{:S(2)}, u32[]{:S(2)}) %all-to-all-start.2) | async-done | bytes 163872 | tf_op jit(solution)/shard_map/all_to_all | solution.py:378
  62.2 4.1 %all-to-all-start.1 = ((f32[8,40,256]{2,1,0:T(8,128)}), f32[8,40,256]{2,1,0:T(8,128)}, u32[]{:S(2)}, u32[]{:S(2)}) async-start(f32[8,40,256]{2,1,0:T(8,128)} %copy-done.10), calls=%async_computation.1 | async-start | bytes 655360 | tf_op jit(solution)/shard_map/all_to_all | solution.py:393
  66.3 1.3 collective-permute-start.12
  67.6 6.0 %collective-permute-start.2 = (f32[128,640]{1,0:T(8,128)}, f32[128,640]{1,0:T(8,128)}, u32[]{:S(2)}, u32[]{:S(2)}) collective-permute-start(f32[128,640]{1,0:T(8,128)} %copy-done.13), channel_id=1, source_target_pairs={{0,16},{1,17},{2,18},{3,19},{4,20},{5,21},{6,22},{7,23},{8,24},{9,... | collective-permute-start | bytes 983048 | tf_op jit(solution)/shard_map/ppermute | solution.py:63
  77.4 5.0 %all-to-all-start.3 = ((f32[8,40,128]{2,1,0:T(8,128)}), f32[8,40,128]{2,1,0:T(8,128)S(1)}, u32[]{:S(2)}, u32[]{:S(2)}) async-start(f32[8,40,128]{2,1,0:T(8,128)} %copy-done.16), calls=%async_computation.3 | async-start | bytes 327680 | tf_op jit(solution)/shard_map/all_to_all | solution.py:393
  83.4 1.6 %shard_map.151 = (f32[2,128,640]{2,1,0:T(8,128)S(1)}, f32[128,640]{1,0:T(8,128)S(1)}) custom-call(s32[2]{0:T(128)S(1)} %pad_add_fusion.place_ref, f32[320,256]{1,0:T(8,128)} %bitcast.11.returned_ref, f32[320,640]{1,0:T(8,128)S(1)} %copy-done.5, f32[2,64,640]{2,1,0:T(8,128)S(1)} %copy-done.20), custom_call_target="tpu_custom_call" | custom-call | flops 209715200 | bytes 2457608 | tf_op jit(solution)/shard_map/pallas_call | solution.py:129
  85.8 1.5 collective-permute-start.1
  90.4 1.3 collective-permute-start.11
  92.3 1.6 collective-permute-start.7
  93.8 9.9 %collective-permute-done.3 = f32[128,640]{1,0:T(8,128)} collective-permute-done((f32[128,640]{1,0:T(8,128)S(1)}, f32[128,640]{1,0:T(8,128)}, u32[]{:S(2)}, u32[]{:S(2)}) %collective-permute-start.3) | collective-permute-done | bytes 327712 | tf_op jit(solution)/shard_map/ppermute | solution.py:44
  111.5 3.9 %collective-permute-done.4 = f32[128,640]{1,0:T(8,128)S(1)} collective-permute-done((f32[128,640]{1,0:T(8,128)S(1)}, f32[128,640]{1,0:T(8,128)S(1)}, u32[]{:S(2)}, u32[]{:S(2)}) %collective-permute-start.4) | collective-permute-done | bytes 327712 | tf_op jit(solution)/shard_map/ppermute | solution.py:63
  116.0 2.5 %copy-done.1 = f32[2048,640]{1,0:T(8,128)S(1)} copy-done((f32[2048,640]{1,0:T(8,128)S(1)}, f32[2048,640]{1,0:T(8,128)}, u32[]{:S(2)}) %copy-start.1) | copy-done | bytes 5242904
  118.5 2.5 %copy-done.3 = f32[640,2048]{1,0:T(8,128)S(1)} copy-done((f32[640,2048]{1,0:T(8,128)S(1)}, f32[640,2048]{1,0:T(8,128)}, u32[]{:S(2)}) %copy-start.3) | copy-done | bytes 5242904
  120.9 6.5 %shard_map.152 = f32[2,128,640]{2,1,0:T(8,128)S(1)} custom-call(s32[2]{0:T(128)S(1)} %pad_add_fusion.place_ref, f32[128,640]{1,0:T(8,128)} %collective-permute-done.2.refs_0_, f32[128,640]{1,0:T(8,128)S(1)} %get-tuple-element.39.refs_1_, f32[128,2048]{1,0:T(8,128)S(1)} %get-tuple-element.28.refs_2_.refs_1_, f32[2048,640]{1,0:T(8,128)S(1)} %copy-done.1, ...), custom_call_target="tpu_custom_call" | custom-call | flops 2684354560 | bytes 12845064 | tf_op jit(solution)/shard_map/pallas_call | solution.py:129
  127.5 1.6 collective-permute-start.5
  129.1 6.8 %shard_map.156 = f32[2,64,640]{2,1,0:T(8,128)S(1)} custom-call(s32[2]{0:T(128)S(1)} %pad_add_fusion.place_ref, f32[128,640]{1,0:T(8,128)S(1)} %add.134.refs_0_, f32[128,2048]{1,0:T(8,128)S(1)} %get-tuple-element.28.refs_2_.refs_1_, f32[2048,640]{1,0:T(8,128)S(1)} %copy-done.1, f32[640,2048]{1,0:T(8,128)S(1)} %copy-done.3), custom_call_target="tpu_custom_call" | custom-call | flops 2013265920 | bytes 12189704 | tf_op jit(solution)/shard_map/pallas_call | solution.py:129
  136.9 5.8 %collective-permute-done.8 = f32[64,640]{1,0:T(8,128)S(1)} collective-permute-done((f32[64,640]{1,0:T(8,128)S(1)}, f32[64,640]{1,0:T(8,128)S(1)}, u32[]{:S(2)}, u32[]{:S(2)}) %collective-permute-start.8) | collective-permute-done | bytes 163872 | tf_op jit(solution)/shard_map/ppermute | solution.py:44
  145.2 1.8 %shard_map.157 = f32[32,128]{1,0:T(8,128)} custom-call(s32[2]{0:T(128)S(1)} %pad_add_fusion.place_ref, f32[128,640]{1,0:T(8,128)S(1)} %copy-done.14, f32[64,640]{1,0:T(8,128)S(1)} %get-tuple-element.41.cov_start_ref, f32[64,640]{1,0:T(8,128)S(1)} %get-tuple-element.36.moved_ref.moved_state_ref, f32[64,640]{1,0:T(8,128)S(1)} %get-tuple-element.37.moved_turn_ref, ...), custom_call_target="tpu_custom_call" | custom-call | flops 1000000 | bytes 3490312 | tf_op jit(solution)/shard_map/pallas_call | solution.py:129
  147.0 4.1 %all-to-all-start.4 = ((f32[32,1,128]{2,1,0:T(1,128)}), f32[32,1,128]{2,1,0:T(1,128)S(1)}, u32[]{:S(2)}, u32[]{:S(2)}) async-start(f32[32,1,128]{2,1,0:T(1,128)} %bitcast.24), calls=%async_computation.4 | async-start | bytes 32768 | tf_op jit(solution)/shard_map/all_to_all | solution.py:510
  152.1 6.2 %all-to-all-done.4 = f32[32,1,128]{2,1,0:T(1,128)S(1)} async-done(((f32[32,1,128]{2,1,0:T(1,128)}), f32[32,1,128]{2,1,0:T(1,128)S(1)}, u32[]{:S(2)}, u32[]{:S(2)}) %all-to-all-start.4) | async-done | bytes 16416 | tf_op jit(solution)/shard_map/all_to_all | solution.py:510
  158.3 1.4 shard_map.158
  (97 shorter events, 37.0 us)
Async XLA Ops:
  2.7 1.1 copy-start.4
  9.0 30.5 %copy-start.11 = (f32[128,640]{1,0:T(8,128)}, f32[128,640]{1,0:T(8,128)S(1)}, u32[]{:S(2)}) copy-start(f32[128,640]{1,0:T(8,128)S(1)} %get-tuple-element.24.rough_ref.push_ref) | copy-start | bytes 983044
  9.0 41.7 %all-to-all-start = ((f32[8,40,256]{2,1,0:T(8,128)}), f32[8,40,256]{2,1,0:T(8,128)S(1)}, u32[]{:S(2)}, u32[]{:S(2)}) async-start(f32[8,40,256]{2,1,0:T(8,128)} %bitcast.8), calls=%async_computation | async-start | bytes 655360 | tf_op jit(solution)/shard_map/all_to_all | solution.py:378
  16.3 11.0 %collective-permute-start = (f32[640,128]{1,0:T(8,128)S(1)}, f32[640,128]{1,0:T(8,128)S(1)}, u32[]{:S(2)}, u32[]{:S(2)}) collective-permute-start(f32[640,128]{1,0:T(8,128)S(1)} %bitcast_convert_fusion), channel_id=1, source_target_pairs={{0,16},{1,17},{2,18},{3,19},{4,20},{5,21},{6,22},{7,23},{8,24},{9,... | collective-permute-start | bytes 983048 | tf_op jit(solution)/shard_map/ppermute | solution.py:217
  27.3 2.5 %copy-start = (f32[2048,640]{1,0:T(8,128)S(1)}, f32[2048,640]{1,0:T(8,128)}, u32[]{:S(2)}) copy-start(f32[2048,640]{1,0:T(8,128)} %refs_2_.3) | copy-start | bytes 15728644
  29.8 2.5 %copy-start.2 = (f32[640,2048]{1,0:T(8,128)S(1)}, f32[640,2048]{1,0:T(8,128)}, u32[]{:S(2)}) copy-start(f32[640,2048]{1,0:T(8,128)} %refs_3_.3) | copy-start | bytes 15728644
  32.3 16.5 %copy-start.5 = (f32[320,640]{1,0:T(8,128)S(1)}, f32[320,640]{1,0:T(8,128)}, u32[]{:S(2)}) copy-start(f32[320,640]{1,0:T(8,128)} %modes_ref.5) | copy-start | bytes 2457604
  39.5 9.3 %copy-start.19 = (f32[2,64,640]{2,1,0:T(8,128)}, f32[2,64,640]{2,1,0:T(8,128)S(1)}, u32[]{:S(2)}) copy-start(f32[2,64,640]{2,1,0:T(8,128)S(1)} %get-tuple-element.25.beside_ref) | copy-start | bytes 983044
  39.5 9.3 %collective-permute-start.6 = (f32[128,640]{1,0:T(8,128)S(1)}, f32[128,640]{1,0:T(8,128)S(1)}, u32[]{:S(2)}, u32[]{:S(2)}) collective-permute-start(f32[128,640]{1,0:T(8,128)S(1)} %get-tuple-element.29.refs_0_), channel_id=1, source_target_pairs={{0,1},{1,0},{2,3},{3,2},{4,5},{5,4},{6,7},{7,6},{8,9},{9,8},{10,11... | collective-permute-start | bytes 983048 | tf_op jit(solution)/shard_map/ppermute | solution.py:44
  50.7 4.4 %copy-start.8 = (f32[8,40,256]{2,1,0:T(8,128)}, f32[8,40,256]{2,1,0:T(8,128)S(1)}, u32[]{:S(2)}) copy-start(f32[8,40,256]{2,1,0:T(8,128)S(1)} %all-to-all-done.owned_ref) | copy-start | bytes 983044
  50.7 11.5 %all-to-all-start.2 = ((f32[8,40,128]{2,1,0:T(8,128)}), f32[8,40,128]{2,1,0:T(8,128)S(1)}, u32[]{:S(2)}, u32[]{:S(2)}) async-start(f32[8,40,128]{2,1,0:T(8,128)} %bitcast.17), calls=%async_computation.2 | async-start | bytes 327680 | tf_op jit(solution)/shard_map/all_to_all | solution.py:378
  62.2 15.2 %all-to-all-start.1 = ((f32[8,40,256]{2,1,0:T(8,128)}), f32[8,40,256]{2,1,0:T(8,128)}, u32[]{:S(2)}, u32[]{:S(2)}) async-start(f32[8,40,256]{2,1,0:T(8,128)} %copy-done.10), calls=%async_computation.1 | async-start | bytes 655360 | tf_op jit(solution)/shard_map/all_to_all | solution.py:393
  66.3 77.8 %collective-permute-start.12 = (f32[128,640]{1,0:T(8,128)}, f32[128,640]{1,0:T(8,128)}, u32[]{:S(2)}, u32[]{:S(2)}) collective-permute-start(f32[128,640]{1,0:T(8,128)} %copy-done.11), channel_id=1, source_target_pairs={{16,0},{17,1},{18,2},{19,3},{20,4},{21,5},{22,6},{23,7},{24,8},{25... | collective-permute-start | bytes 983048 | tf_op jit(solution)/shard_map/ppermute | solution.py:63
  67.6 21.7 %collective-permute-start.2 = (f32[128,640]{1,0:T(8,128)}, f32[128,640]{1,0:T(8,128)}, u32[]{:S(2)}, u32[]{:S(2)}) collective-permute-start(f32[128,640]{1,0:T(8,128)} %copy-done.13), channel_id=1, source_target_pairs={{0,16},{1,17},{2,18},{3,19},{4,20},{5,21},{6,22},{7,23},{8,24},{9,... | collective-permute-start | bytes 983048 | tf_op jit(solution)/shard_map/ppermute | solution.py:63
  77.4 14.3 %all-to-all-start.3 = ((f32[8,40,128]{2,1,0:T(8,128)}), f32[8,40,128]{2,1,0:T(8,128)S(1)}, u32[]{:S(2)}, u32[]{:S(2)}) async-start(f32[8,40,128]{2,1,0:T(8,128)} %copy-done.16), calls=%async_computation.3 | async-start | bytes 327680 | tf_op jit(solution)/shard_map/all_to_all | solution.py:393
  85.0 4.3 %copy-start.15 = (f32[2,128,640]{2,1,0:T(8,128)}, f32[2,128,640]{2,1,0:T(8,128)S(1)}, u32[]{:S(2)}) copy-start(f32[2,128,640]{2,1,0:T(8,128)S(1)} %get-tuple-element.26) | copy-start | bytes 1966084
  85.8 19.9 %collective-permute-start.1 = (f32[128,640]{1,0:T(8,128)}, f32[128,640]{1,0:T(8,128)}, u32[]{:S(2)}, u32[]{:S(2)}) collective-permute-start(f32[128,640]{1,0:T(8,128)} %slice_bitcast_fusion.2), channel_id=1, source_target_pairs={{0,1},{1,0},{2,3},{3,2},{4,5},{5,4},{6,7},{7,6},{8,9},{9,8},{10,11... | collective-permute-start | bytes 983048 | tf_op jit(solution)/shard_map/ppermute | solution.py:44
  87.3 16.4 %collective-permute-start.3 = (f32[128,640]{1,0:T(8,128)S(1)}, f32[128,640]{1,0:T(8,128)}, u32[]{:S(2)}, u32[]{:S(2)}) collective-permute-start(f32[128,640]{1,0:T(8,128)S(1)} %get-tuple-element.27), channel_id=1, source_target_pairs={{0,1},{1,0},{2,3},{3,2},{4,5},{5,4},{6,7},{7,6},{8,9},{9,8},{10,11... | collective-permute-start | bytes 983048 | tf_op jit(solution)/shard_map/ppermute | solution.py:44
  90.4 53.7 %collective-permute-start.11 = (f32[128,640]{1,0:T(8,128)}, f32[128,640]{1,0:T(8,128)S(1)}, u32[]{:S(2)}, u32[]{:S(2)}) collective-permute-start(f32[128,640]{1,0:T(8,128)} %copy-done.21), channel_id=1, source_target_pairs={{16,0},{17,1},{18,2},{19,3},{20,4},{21,5},{22,6},{23,7},{24,8},{25... | collective-permute-start | bytes 983048 | tf_op jit(solution)/shard_map/ppermute | solution.py:63
  92.3 17.9 %collective-permute-start.7 = (f32[128,640]{1,0:T(8,128)S(1)}, f32[128,640]{1,0:T(8,128)S(1)}, u32[]{:S(2)}, u32[]{:S(2)}) collective-permute-start(f32[128,640]{1,0:T(8,128)S(1)} %shard_map.155), channel_id=1, source_target_pairs={{0,1},{1,0},{2,3},{3,2},{4,5},{5,4},{6,7},{7,6},{8,9},{9,8},{10,11... | collective-permute-start | bytes 983048 | tf_op jit(solution)/shard_map/ppermute | solution.py:44
  104.7 10.6 %collective-permute-start.4 = (f32[128,640]{1,0:T(8,128)S(1)}, f32[128,640]{1,0:T(8,128)S(1)}, u32[]{:S(2)}, u32[]{:S(2)}) collective-permute-start(f32[128,640]{1,0:T(8,128)S(1)} %add.131), channel_id=1, source_target_pairs={{0,16},{16,0},{1,17},{17,1},{2,18},{18,2},{3,19},{19,3},{4,20},{20... | collective-permute-start | bytes 983048 | tf_op jit(solution)/shard_map/ppermute | solution.py:63
  107.8 37.4 %collective-permute-start.10 = (f32[128,640]{1,0:T(8,128)S(1)}, f32[128,640]{1,0:T(8,128)S(1)}, u32[]{:S(2)}, u32[]{:S(2)}) collective-permute-start(f32[128,640]{1,0:T(8,128)S(1)} %pad_maximum_fusion.1), channel_id=1, source_target_pairs={{16,0},{17,1},{18,2},{19,3},{20,4},{21,5},{22,6},{23,7},{24,8},{25... | collective-permute-start | bytes 983048 | tf_op jit(solution)/shard_map/ppermute | solution.py:63
  110.2 34.9 %collective-permute-start.9 = (f32[128,640]{1,0:T(8,128)S(1)}, f32[128,640]{1,0:T(8,128)S(1)}, u32[]{:S(2)}, u32[]{:S(2)}) collective-permute-start(f32[128,640]{1,0:T(8,128)S(1)} %add.134.refs_0_), channel_id=1, source_target_pairs={{16,0},{17,1},{18,2},{19,3},{20,4},{21,5},{22,6},{23,7},{24,8},{25... | collective-permute-start | bytes 983048 | tf_op jit(solution)/shard_map/ppermute | solution.py:63
  116.0 2.5 %copy-start.1 = (f32[2048,640]{1,0:T(8,128)S(1)}, f32[2048,640]{1,0:T(8,128)}, u32[]{:S(2)}) copy-start(f32[2048,640]{1,0:T(8,128)} %refs_2_.3) | copy-start | bytes 15728644
  118.5 2.5 %copy-start.3 = (f32[640,2048]{1,0:T(8,128)S(1)}, f32[640,2048]{1,0:T(8,128)}, u32[]{:S(2)}) copy-start(f32[640,2048]{1,0:T(8,128)} %refs_3_.3) | copy-start | bytes 15728644
  127.5 16.6 %copy-start.12 = (f32[128,640]{1,0:T(8,128)S(1)}, f32[128,640]{1,0:T(8,128)}, u32[]{:S(2)}) copy-start(f32[128,640]{1,0:T(8,128)} %copy-done.11) | copy-start | bytes 983044
  127.5 17.7 %copy-start.7 = (f32[1,64,640]{2,1,0:T(8,128)S(1)}, f32[1,64,640]{2,1,0:T(8,128)}, u32[]{:S(2)}) copy-start(f32[1,64,640]{2,1,0:T(8,128)} %param.14) | copy-start | bytes 491524
  127.5 8.4 %collective-permute-start.5 = (f32[128,640]{1,0:T(8,128)S(1)}, f32[128,640]{1,0:T(8,128)S(1)}, u32[]{:S(2)}, u32[]{:S(2)}) collective-permute-start(f32[128,640]{1,0:T(8,128)S(1)} %slice_bitcast_fusion), channel_id=1, source_target_pairs={{0,1},{1,0},{2,3},{3,2},{4,5},{5,4},{6,7},{7,6},{8,9},{9,8},{10,11... | collective-permute-start | bytes 983048 | tf_op jit(solution)/shard_map/ppermute | solution.py:44
  135.9 9.3 %copy-start.14 = (f32[128,640]{1,0:T(8,128)S(1)}, f32[128,640]{1,0:T(8,128)}, u32[]{:S(2)}) copy-start(f32[128,640]{1,0:T(8,128)} %copy-done.13) | copy-start | bytes 983044
  135.9 6.8 %collective-permute-start.8 = (f32[64,640]{1,0:T(8,128)S(1)}, f32[64,640]{1,0:T(8,128)S(1)}, u32[]{:S(2)}, u32[]{:S(2)}) collective-permute-start(f32[64,640]{1,0:T(8,128)S(1)} %slice_bitcast_fusion.3), channel_id=1, source_target_pairs={{0,1},{1,0},{2,3},{3,2},{4,5},{5,4},{6,7},{7,6},{8,9},{9,8},{10,11... | collective-permute-start | bytes 491528 | tf_op jit(solution)/shard_map/ppermute | solution.py:44
  142.8 8.3 %collective-permute-start.13 = (f32[64,640]{1,0:T(8,128)S(1)}, f32[64,640]{1,0:T(8,128)}, u32[]{:S(2)}, u32[]{:S(2)}) collective-permute-start(f32[64,640]{1,0:T(8,128)S(1)} %get-tuple-element.36.moved_ref.moved_state_ref), channel_id=1, source_target_pairs={{0,1},{1,0},{2,3},{3,2},{4,5},{5,4},{6,7},{7,6},{8,9},{9,8},{10,11... | collective-permute-start | bytes 491528 | tf_op jit(solution)/shard_map/ppermute | solution.py:44
  147.0 11.3 %all-to-all-start.4 = ((f32[32,1,128]{2,1,0:T(1,128)}), f32[32,1,128]{2,1,0:T(1,128)S(1)}, u32[]{:S(2)}, u32[]{:S(2)}) async-start(f32[32,1,128]{2,1,0:T(1,128)} %bitcast.24), calls=%async_computation.4 | async-start | bytes 32768 | tf_op jit(solution)/shard_map/all_to_all | solution.py:510
  (9 other events, 7.7 us)

commit v3 on v2

--- a/solution.py
+++ b/solution.py
@@ -69,10 +69,9 @@
             if not used or used == {0.0}:
                 continue
             if len(used) > 1:
-                factors = np.zeros(size, np.float32)
-                for dest, source in cells[distance]:
-                    factors[dest] = weights[dest, source]
-                block = block * jnp.asarray(factors)[here]
+                block = block * sum(
+                    float(weights[dest, source]) * (here == dest).astype(F32) for dest, source in cells[distance]
+                )
             elif used != {1.0}:
                 block = block * used.pop()
             total = block if total is None else total + block
@@ -182,9 +181,9 @@
     first = (0,)
     place = jnp.stack([group_index, here]).astype(jnp.int32)
 
-    def turned(place_ref, ref, value):
-        for step in range(groups):
-            ref[step] = value_rows(value, lax.rem(place_ref[0] + step, groups))
+    def turned(place_ref, outs, value):
+        for step, ref in enumerate(outs):
+            ref[...] = value_rows(value, lax.rem(place_ref[0] + step, groups))
 
     def value_rows(value, index):
         total = value[:rows]
@@ -248,6 +247,7 @@
         [start_mult[0], first_rhs[0], data, variance, pick, vertical_modes],
         8 * half_modes * depth * width,
     )
+    weights = [pltpu.with_memory_space_constraint(w, pltpu.HBM) for w in (weight_in, weight_out)]
     whole_spec = [pl.BlockSpec(memory_space=pltpu.SMEM)]
 
     def fixed(*dims):
@@ -257,7 +257,8 @@
     out_block = pl.BlockSpec((depth, block), lambda i: (0, i))
     slope_block = pl.BlockSpec((width, block), lambda i: (0, i))
 
-    def slopes_and_adjoint(place_ref, fine_ref, rough_ref, before_ref, win_ref, wout_ref, fine_out, rough_out, slopes_ref, total_ref, turned_ref):
+    def slopes_and_adjoint(place_ref, fine_ref, rough_ref, before_ref, win_ref, wout_ref, fine_out, *rest):
+        rough_outs, (slopes_ref, total_ref, turned_ref) = rest[:groups], rest[groups:]
         index = pl.program_id(0)
 
         @pl.when(index == 0)
@@ -278,18 +279,18 @@
         @pl.when(index == steps - 1)
         def _():
             fine_out[...] = total_ref[:width]
-            turned(place_ref, rough_out, total_ref[width:])
+            turned(place_ref, rough_outs, total_ref[width:])
 
     push_fed, push_later = mixtures(push, [(later, first, ()), (later, (), ())])
-    pull0_part, pull2_parts, slopes = call(
+    pull0_part, *pull2_parts, slopes = call(
         slopes_and_adjoint,
-        [shape(width, depth), shape(groups, rows, depth), shape(width, hidden)],
-        [place, start, push_fed, before, weight_in, weight_out],
+        [shape(width, depth)] + [shape(rows, depth)] * groups + [shape(width, hidden)],
+        [place, start, push_fed, before, *weights],
         20 * hidden * depth * width,
         vmem_mib=20,
         grid=(steps,),
         in_specs=whole_spec + [fixed(width, depth)] * 2 + [fixed(depth, width), in_block, out_block],
-        out_specs=[fixed(width, depth), fixed(groups, rows, depth), slope_block],
+        out_specs=[fixed(width, depth)] + [fixed(rows, depth)] * groups + [slope_block],
         scratch=[pltpu.VMEM((2 * width, depth), F32), pltpu.VMEM((width, depth), BF16)],
     )
 
@@ -305,7 +306,7 @@
         return call(
             kernel,
             shape(width, depth),
-            [field, slopes, weight_in, weight_out],
+            [field, slopes, *weights],
             12 * hidden * depth * width,
             vmem_mib=20,
             grid=(steps,),
@@ -317,7 +318,7 @@
         count = 1 if rough is None else 2
 
         def kernel(place_ref, *refs):
-            fields, (slopes_ref, win_ref, wout_ref, out_ref, total_ref) = refs[:count], refs[count:]
+            fields, (slopes_ref, win_ref, wout_ref, *outs, total_ref) = refs[:count], refs[count:]
 
             @pl.when(pl.program_id(0) == 0)
             def _():
@@ -333,19 +334,19 @@
                 for i in range(count):
                     turned(
                         place_ref,
-                        out_ref.at[:, i * rows : (i + 1) * rows],
+                        [out.at[i * rows : (i + 1) * rows] for out in outs],
                         total_ref[i * width : (i + 1) * width],
                     )
 
         parts = call(
             kernel,
-            shape(groups, count * rows, depth),
-            [place, fine, *([] if rough is None else [rough]), slopes, weight_in, weight_out],
+            [shape(count * rows, depth)] * groups,
+            [place, fine, *([] if rough is None else [rough]), slopes, *weights],
             (12 if rough is None else 16) * hidden * depth * width,
             vmem_mib=20,
             grid=(steps,),
             in_specs=whole_spec + [fixed(width, depth)] * count + [slope_block, in_block, out_block],
-            out_specs=fixed(groups, count * rows, depth),
+            out_specs=[fixed(count * rows, depth)] * groups,
             scratch=[pltpu.VMEM((count * width, depth), F32)],
         )
         return summed_own(parts)
@@ -400,17 +401,20 @@
         return call(kernel, shape(width, depth), [returned, vertical_modes], 6 * half_modes * depth * width)
 
     def back_to_columns_early(returned, beside):
-        def kernel(place_ref, returned_ref, modes_ref, beside_ref, rough_out, fine_out):
+        def kernel(place_ref, returned_ref, modes_ref, *refs):
+            beside_refs, rough_outs, fine_out = refs[:groups], refs[groups:-1], refs[-1]
             modes = halves(modes_ref[...])
             back = returned_ref[...].T
-            turned(place_ref, rough_out.at[:, :rows], contract(back[:width].astype(BF16), modes[0], (1, 0)))
-            rough_out[:, rows:] = beside_ref[...]
+            rough = contract(back[:width].astype(BF16), modes[0], (1, 0))
+            turned(place_ref, [out.at[:rows] for out in rough_outs], rough)
+            for beside_ref, out in zip(beside_refs, rough_outs):
+                out[rows:] = beside_ref[...]
             fine_out[...] = contract3(halves(back[width:]), modes, (1, 0))
 
         return call(
             kernel,
-            [shape(groups, 2 * rows, depth), shape(width, depth)],
-            [place, returned, vertical_modes, beside],
+            [shape(2 * rows, depth)] * groups + [shape(width, depth)],
+            [place, returned, vertical_modes, *beside],
             8 * half_modes * depth * width,
         )
 
@@ -419,7 +423,7 @@
         return summed(back_to_columns(correlated(amp)))
 
     pull0, amp_pull = amplitudes([pull0_part, *sent(pull0_part)])
-    beside_parts, cov_push_part = back_to_columns_early(correlated(amp_early), pull2_parts)
+    *beside_parts, cov_push_part = back_to_columns_early(correlated(amp_early), pull2_parts)
     cov_push = summed(cov_push_part)
     push_feed, push_state = mixtures(cov_push, [(down @ earlier @ later, first, ()), (earlier @ later, (), ())])
     rhs_feed, rhs_state = mixtures(rhs, [(down @ earlier, first, ()), (earlier, (), ())])

time: 161 us -> 154 us (0.957)
  local copies, waits for them, and re-layouts: 25.4 us -> 16.6 us
  Pallas kernels: 31.6 us -> 37.6 us
  other arithmetic: 11.2 us -> 9.55 us
    pallas_call x11, Pallas kernels: 31.6 us -> 37.6 us  [call(): pl.pallas_call(kernel, out_shape=out, grid=grid or (), in_specs=in_specs,...]
    ppermute x1, waiting for transfers between devices: 5.67 us -> 0.01 us  [on_device(): lax.ppermute(trajectory[0].astype(F32), 'sub', [(i, i + 1) for i in range...]
    ppermute x6, waiting for transfers between devices: 3.88 us -> 9.4 us  [mixtures(): lax.ppermute(field, 'sub', [(source, dest) for dest, source in cells[dist...]
    unnamed x44 -> x46, local copies, waits for them, and re-layouts: 18.8 us -> 14.2 us
    ppermute x7, waiting for transfers between devices: 23.4 us -> 19.2 us  [rotated(): lax.ppermute(block, axis, [(i, (i + distance) % size) for i in range(size)])]
    all_to_all x2, waiting for transfers between devices: 2.25 us -> 4.65 us  [correlated(): lax.all_to_all(amp.reshape(shards, owned_modes, count * width), 'col', 0,...]
    add x5, other arithmetic: 3.22 us -> 5 us  [plus(): return sum(kept[1:], kept[0]) if kept else None]
  transfers between devices with their start and end apart: 19 -> 19, of which waited for: 8 -> 9; matrix products, arithmetic and copies ran while one was open for 10% -> 7% of each run, Pallas kernels for 18% -> 23%
where the time goes in v3:
time: 154 us; the launch traced here: 153 us
  starting transfers between devices  46.7 us (30%)
  waiting for transfers between devices  40.4 us (26%)
  Pallas kernels  37.6 us (24%)
  local copies, waits for them, and re-layouts  16.6 us (11%)
  other arithmetic  9.55 us (6%)
  between operations  1.71 us (1%)
    pallas_call x11, Pallas kernels, call(): pl.pallas_call(kernel, out_shape=out, grid=grid or (), in_specs=in_specs,...  37.6 us
    ppermute x7, waiting for transfers between devices, rotated(): lax.ppermute(block, axis, [(i, (i + distance) % size) for i in range(size)])  19.2 us
    unnamed x46, local copies, waits for them, and re-layouts  14.2 us
    all_to_all x2, starting transfers between devices, correlated(): lax.all_to_all(amp.reshape(shards, owned_modes, count * width), 'col', 0,...  11.1 us
    ppermute x6, starting transfers between devices, mixtures(): lax.ppermute(field, 'sub', [(source, dest) for dest, source in cells[dist...  10.9 us
    ppermute x6, waiting for transfers between devices, mixtures(): lax.ppermute(field, 'sub', [(source, dest) for dest, source in cells[dist...  9.4 us
    all_to_all x2, starting transfers between devices, correlated(): returned = lax.all_to_all(back, 'col', 0, 0, tiled=True)  9.04 us
    ppermute x7, starting transfers between devices, rotated(): lax.ppermute(block, axis, [(i, (i + distance) % size) for i in range(size)])  8.89 us
  transfers between devices with their start and end apart: 19, of which 9 were waited for; matrix products, arithmetic and copies ran while one was open for 7% of the time, Pallas kernels for 23%

profile of v3, /device:TPU:0, one launch (start us, length us, event | category | flops | bytes accessed | tf_op | source)
XLA Modules:
  0.0 152.6 jit_solution(18131292222691121762)
XLA Ops:
  6.8 1.5 shard_map.139
  9.8 6.4 %all-to-all-start = ((f32[8,40,256]{2,1,0:T(8,128)}), f32[8,40,256]{2,1,0:T(8,128)S(1)}, u32[]{:S(2)}, u32[]{:S(2)}) async-start(f32[8,40,256]{2,1,0:T(8,128)} %bitcast.8), calls=%async_computation | async-start | bytes 655360 | tf_op jit(solution)/shard_map/all_to_all | solution.py:379
  17.0 3.4 %collective-permute-start = (f32[640,128]{1,0:T(8,128)S(1)}, f32[640,128]{1,0:T(8,128)S(1)}, u32[]{:S(2)}, u32[]{:S(2)}) collective-permute-start(f32[640,128]{1,0:T(8,128)S(1)} %bitcast_convert_fusion), channel_id=1, source_target_pairs={{0,16},{1,17},{2,18},{3,19},{4,20},{5,21},{6,22},{7,23},{8,24},{9,... | collective-permute-start | bytes 983048 | tf_op jit(solution)/shard_map/ppermute | solution.py:216
  22.7 4.5 %all-to-all-done.owned_ref = f32[8,40,256]{2,1,0:T(8,128)S(1)} async-done(((f32[8,40,256]{2,1,0:T(8,128)}), f32[8,40,256]{2,1,0:T(8,128)S(1)}, u32[]{:S(2)}, u32[]{:S(2)}) %all-to-all-start) | async-done | bytes 327712 | tf_op jit(solution)/shard_map/all_to_all | solution.py:379
  27.2 2.6 %shard_map.140 = f32[8,40,256]{2,1,0:T(8,128)} custom-call(f32[8,40,256]{2,1,0:T(8,128)S(1)} %all-to-all-done.owned_ref, f32[1024,256]{1,0:T(8,128)S(1)} %pad_maximum_fusion.table_ref, f32[40,256]{1,0:T(8,128)S(1)} %pad_maximum_fusion.2.spec_ref), custom_call_target="tpu_custom_call" | custom-call | flops 251658240 | bytes 1744896 | tf_op jit(solution)/shard_map/pallas_call | solution.py:128
  29.8 4.1 %all-to-all-start.1 = ((f32[8,40,256]{2,1,0:T(8,128)}), f32[8,40,256]{2,1,0:T(8,128)}, u32[]{:S(2)}, u32[]{:S(2)}) async-start(f32[8,40,256]{2,1,0:T(8,128)} %shard_map.140), calls=%async_computation.1 | async-start | bytes 655360 | tf_op jit(solution)/shard_map/all_to_all | solution.py:394
  36.6 8.4 %shard_map.141 = (f32[128,640]{1,0:T(8,128)S(1)}, f32[64,640]{1,0:T(8,128)S(1)}, f32[64,640]{1,0:T(8,128)S(1)}, f32[128,2048]{1,0:T(8,128)S(1)}) custom-call(s32[2]{0:T(128)S(1)} %pad_add_fusion.place_ref, f32[128,640]{1,0:T(8,128)S(1)} %get-tuple-element.29.fine_ref.start_ref, f32[128,640]{1,0:T(8,128)S(1)} %copy-done.5, f32[640,128]{1,0:T(8,128)S(1)} %copy-done.22, ...), custom_call_target="tpu_custom_call" | custom-call | flops 3355443200 | bytes 13172744 | tf_op jit(solution)/shard_map/pallas_call | solution.py:128
  46.3 1.5 collective-permute-start.6
  47.8 8.5 %collective-permute-done.6.refs_1_ = f32[128,640]{1,0:T(8,128)S(1)} collective-permute-done((f32[128,640]{1,0:T(8,128)S(1)}, f32[128,640]{1,0:T(8,128)S(1)}, u32[]{:S(2)}, u32[]{:S(2)}) %collective-permute-start.6) | collective-permute-done | bytes 327712 | tf_op jit(solution)/shard_map/ppermute | solution.py:44
  58.2 4.7 %all-to-all-start.2 = ((f32[8,40,128]{2,1,0:T(8,128)}), f32[8,40,128]{2,1,0:T(8,128)}, u32[]{:S(2)}, u32[]{:S(2)}) async-start(f32[8,40,128]{2,1,0:T(8,128)} %bitcast.13), calls=%async_computation.2 | async-start | bytes 327680 | tf_op jit(solution)/shard_map/all_to_all | solution.py:379
  64.8 2.3 %shard_map.142 = (f32[128,640]{1,0:T(8,128)S(1)}, f32[128,640]{1,0:T(8,128)S(1)}, f32[128,640]{1,0:T(8,128)}) custom-call(s32[2]{0:T(128)S(1)} %pad_add_fusion.place_ref, f32[320,256]{1,0:T(8,128)} %bitcast.11.returned_ref, f32[320,640]{1,0:T(8,128)S(1)} %copy-done.1, f32[64,640]{1,0:T(8,128)S(1)} %copy-done.16, f32[64,640]{1,0:T(8,128)S(1)} %copy-done.18), custom_call_target="tpu_custom_call" | custom-call | flops 209715200 | bytes 2457608 | tf_op jit(solution)/shard_map/pallas_call | solution.py:128
  68.6 1.5 collective-permute-start.3
  70.2 2.1 %shard_map.145 = f32[8,40,128]{2,1,0:T(8,128)S(1)} custom-call(f32[8,40,128]{2,1,0:T(8,128)} %all-to-all-done.2.owned_ref, f32[1024,256]{1,0:T(8,128)S(1)} %pad_maximum_fusion.table_ref, f32[40,256]{1,0:T(8,128)S(1)} %pad_maximum_fusion.2.spec_ref), custom_call_target="tpu_custom_call" | custom-call | flops 125829120 | bytes 1417216 | tf_op jit(solution)/shard_map/pallas_call | solution.py:128
  73.1 5.0 %all-to-all-start.3 = ((f32[8,40,128]{2,1,0:T(8,128)}), f32[8,40,128]{2,1,0:T(8,128)S(1)}, u32[]{:S(2)}, u32[]{:S(2)}) async-start(f32[8,40,128]{2,1,0:T(8,128)} %copy-done.11), calls=%async_computation.3 | async-start | bytes 327680 | tf_op jit(solution)/shard_map/all_to_all | solution.py:394
  79.3 5.3 %collective-permute-start.2 = (f32[128,640]{1,0:T(8,128)}, f32[128,640]{1,0:T(8,128)S(1)}, u32[]{:S(2)}, u32[]{:S(2)}) collective-permute-start(f32[128,640]{1,0:T(8,128)} %copy-done.7), channel_id=1, source_target_pairs={{0,16},{1,17},{2,18},{3,19},{4,20},{5,21},{6,22},{7,23},{8,24},{9,... | collective-permute-start | bytes 983048 | tf_op jit(solution)/shard_map/ppermute | solution.py:63
  85.8 1.6 %collective-permute-start.7 = (f32[128,640]{1,0:T(8,128)S(1)}, f32[128,640]{1,0:T(8,128)}, u32[]{:S(2)}, u32[]{:S(2)}) collective-permute-start(f32[128,640]{1,0:T(8,128)S(1)} %shard_map.146), channel_id=1, source_target_pairs={{0,1},{1,0},{2,3},{3,2},{4,5},{5,4},{6,7},{7,6},{8,9},{9,8},{10,11... | collective-permute-start | bytes 983048 | tf_op jit(solution)/shard_map/ppermute | solution.py:44
  87.4 1.8 %add.131 = f32[128,640]{1,0:T(8,128)} add(f32[128,640]{1,0:T(8,128)} %get-tuple-element.35, f32[128,640]{1,0:T(8,128)} %collective-permute-done.3) | non-fusion elementwise | flops 81920 | bytes 983040 | tf_op jit(solution)/shard_map/add | solution.py:84
  89.7 3.2 %collective-permute-done.2.refs_0_ = f32[128,640]{1,0:T(8,128)S(1)} collective-permute-done((f32[128,640]{1,0:T(8,128)}, f32[128,640]{1,0:T(8,128)S(1)}, u32[]{:S(2)}, u32[]{:S(2)}) %collective-permute-start.2) | collective-permute-done | bytes 327712 | tf_op jit(solution)/shard_map/ppermute | solution.py:63
  94.0 1.3 collective-permute-start.11
  96.7 4.9 %collective-permute-done.7 = f32[128,640]{1,0:T(8,128)} collective-permute-done((f32[128,640]{1,0:T(8,128)S(1)}, f32[128,640]{1,0:T(8,128)}, u32[]{:S(2)}, u32[]{:S(2)}) %collective-permute-start.7) | collective-permute-done | bytes 327712 | tf_op jit(solution)/shard_map/ppermute | solution.py:44
  102.6 8.0 %shard_map.147 = (f32[64,640]{1,0:T(8,128)S(1)}, f32[64,640]{1,0:T(8,128)S(1)}) custom-call(s32[2]{0:T(128)S(1)} %pad_add_fusion.place_ref, f32[128,640]{1,0:T(8,128)S(1)} %add.134.refs_0_, f32[128,2048]{1,0:T(8,128)S(1)} %get-tuple-element.36.refs_2_.refs_1_, f32[2048,640]{1,0:T(8,128)} %refs_2_.3, f32[640,2048]{1,0:T(8,128)} %refs_3_.3), custom_call_target="tpu_custom_call" | custom-call | flops 2013265920 | bytes 12189704 | tf_op jit(solution)/shard_map/pallas_call | solution.py:128
  112.4 7.6 %shard_map.143 = (f32[128,640]{1,0:T(8,128)S(1)}, f32[128,640]{1,0:T(8,128)S(1)}) custom-call(s32[2]{0:T(128)S(1)} %pad_add_fusion.place_ref, f32[128,640]{1,0:T(8,128)S(1)} %collective-permute-done.2.refs_0_, f32[128,640]{1,0:T(8,128)S(1)} %get-tuple-element.50.refs_1_, f32[128,2048]{1,0:T(8,128)S(1)} %get-tuple-element.36.refs_2_.refs_1_, ...), custom_call_target="tpu_custom_call" | custom-call | flops 2684354560 | bytes 12845064 | tf_op jit(solution)/shard_map/pallas_call | solution.py:128
  120.0 1.6 %collective-permute-start.5 = (f32[128,640]{1,0:T(8,128)S(1)}, f32[128,640]{1,0:T(8,128)S(1)}, u32[]{:S(2)}, u32[]{:S(2)}) collective-permute-start(f32[128,640]{1,0:T(8,128)S(1)} %get-tuple-element.38), channel_id=1, source_target_pairs={{0,1},{1,0},{2,3},{3,2},{4,5},{5,4},{6,7},{7,6},{8,9},{9,8},{10,11... | collective-permute-start | bytes 983048 | tf_op jit(solution)/shard_map/ppermute | solution.py:44
  121.7 1.3 collective-permute-start.10
  123.0 5.5 %collective-permute-done.5 = f32[128,640]{1,0:T(8,128)S(1)} collective-permute-done((f32[128,640]{1,0:T(8,128)S(1)}, f32[128,640]{1,0:T(8,128)S(1)}, u32[]{:S(2)}, u32[]{:S(2)}) %collective-permute-start.5) | collective-permute-done | bytes 327712 | tf_op jit(solution)/shard_map/ppermute | solution.py:44
  128.5 1.3 collective-permute-start.9
  129.9 1.6 %collective-permute-start.13 = (f32[64,640]{1,0:T(8,128)S(1)}, f32[64,640]{1,0:T(8,128)S(1)}, u32[]{:S(2)}, u32[]{:S(2)}) collective-permute-start(f32[64,640]{1,0:T(8,128)S(1)} %get-tuple-element.48.moved_ref.moved_state_ref), channel_id=1, source_target_pairs={{0,1},{1,0},{2,3},{3,2},{4,5},{5,4},{6,7},{7,6},{8,9},{9,8},{10,11... | collective-permute-start | bytes 491528 | tf_op jit(solution)/shard_map/ppermute | solution.py:44
  132.5 6.2 %collective-permute-done.9 = f32[128,640]{1,0:T(8,128)S(1)} collective-permute-done((f32[128,640]{1,0:T(8,128)S(1)}, f32[128,640]{1,0:T(8,128)S(1)}, u32[]{:S(2)}, u32[]{:S(2)}) %collective-permute-start.9) | collective-permute-done | bytes 327712 | tf_op jit(solution)/shard_map/ppermute | solution.py:63
  138.8 1.8 %shard_map.148 = f32[32,128]{1,0:T(8,128)} custom-call(s32[2]{0:T(128)S(1)} %pad_add_fusion.place_ref, f32[128,640]{1,0:T(8,128)S(1)} %copy-done.8, f32[64,640]{1,0:T(8,128)S(1)} %get-tuple-element.53.cov_start_ref, f32[64,640]{1,0:T(8,128)S(1)} %get-tuple-element.48.moved_ref.moved_state_ref, f32[64,640]{1,0:T(8,128)S(1)} %get-tuple-element.51.moved_turn_ref, ...), custom_call_target="tpu_custom_call" | custom-call | flops 1000000 | bytes 3490312 | tf_op jit(solution)/shard_map/pallas_call | solution.py:128
  140.6 3.4 %all-to-all-start.4 = ((f32[32,1,128]{2,1,0:T(1,128)}), f32[32,1,128]{2,1,0:T(1,128)S(1)}, u32[]{:S(2)}, u32[]{:S(2)}) async-start(f32[32,1,128]{2,1,0:T(1,128)} %bitcast.17), calls=%async_computation.4 | async-start | bytes 32768 | tf_op jit(solution)/shard_map/all_to_all | solution.py:514
  144.1 7.1 %all-to-all-done.4 = f32[32,1,128]{2,1,0:T(1,128)S(1)} async-done(((f32[32,1,128]{2,1,0:T(1,128)}), f32[32,1,128]{2,1,0:T(1,128)S(1)}, u32[]{:S(2)}, u32[]{:S(2)}) %all-to-all-start.4) | async-done | bytes 16416 | tf_op jit(solution)/shard_map/all_to_all | solution.py:514
  151.2 1.4 shard_map.149
  (95 shorter events, 29.4 us)
Async XLA Ops:
  2.7 5.6 %copy-start.9 = (f32[128,64]{1,0:T(8,128)}, f32[128,64]{1,0:T(8,128)S(1)}, u32[]{:S(2)}) copy-start(f32[128,64]{1,0:T(8,128)S(1)} %fusion.pick_ref) | copy-start | bytes 98308
  2.7 1.2 copy-start
  3.9 0.9 copy-start.2
  4.8 1.0 copy-start.12
  5.8 1.0 copy-start.13
  9.8 17.5 %all-to-all-start = ((f32[8,40,256]{2,1,0:T(8,128)}), f32[8,40,256]{2,1,0:T(8,128)S(1)}, u32[]{:S(2)}, u32[]{:S(2)}) async-start(f32[8,40,256]{2,1,0:T(8,128)} %bitcast.8), calls=%async_computation | async-start | bytes 655360 | tf_op jit(solution)/shard_map/all_to_all | solution.py:379
  17.0 16.8 %collective-permute-start = (f32[640,128]{1,0:T(8,128)S(1)}, f32[640,128]{1,0:T(8,128)S(1)}, u32[]{:S(2)}, u32[]{:S(2)}) collective-permute-start(f32[640,128]{1,0:T(8,128)S(1)} %bitcast_convert_fusion), channel_id=1, source_target_pairs={{0,16},{1,17},{2,18},{3,19},{4,20},{5,21},{6,22},{7,23},{8,24},{9,... | collective-permute-start | bytes 983048 | tf_op jit(solution)/shard_map/ppermute | solution.py:216
  29.8 28.4 %all-to-all-start.1 = ((f32[8,40,256]{2,1,0:T(8,128)}), f32[8,40,256]{2,1,0:T(8,128)}, u32[]{:S(2)}, u32[]{:S(2)}) async-start(f32[8,40,256]{2,1,0:T(8,128)} %shard_map.140), calls=%async_computation.1 | async-start | bytes 655360 | tf_op jit(solution)/shard_map/all_to_all | solution.py:394
  34.6 1.0 copy-start.5
  35.6 1.0 copy-start.22
  36.6 19.7 %copy-start.1 = (f32[320,640]{1,0:T(8,128)S(1)}, f32[320,640]{1,0:T(8,128)}, u32[]{:S(2)}) copy-start(f32[320,640]{1,0:T(8,128)} %modes_ref.5) | copy-start | bytes 2457604
  46.3 10.0 %collective-permute-start.6 = (f32[128,640]{1,0:T(8,128)S(1)}, f32[128,640]{1,0:T(8,128)S(1)}, u32[]{:S(2)}, u32[]{:S(2)}) collective-permute-start(f32[128,640]{1,0:T(8,128)S(1)} %get-tuple-element.39.refs_0_), channel_id=1, source_target_pairs={{0,1},{1,0},{2,3},{3,2},{4,5},{5,4},{6,7},{7,6},{8,9},{9,8},{10,11... | collective-permute-start | bytes 983048 | tf_op jit(solution)/shard_map/ppermute | solution.py:44
  58.2 12.0 %all-to-all-start.2 = ((f32[8,40,128]{2,1,0:T(8,128)}), f32[8,40,128]{2,1,0:T(8,128)}, u32[]{:S(2)}, u32[]{:S(2)}) async-start(f32[8,40,128]{2,1,0:T(8,128)} %bitcast.13), calls=%async_computation.2 | async-start | bytes 327680 | tf_op jit(solution)/shard_map/all_to_all | solution.py:379
  62.9 0.9 copy-start.16
  68.6 18.8 %collective-permute-start.3 = (f32[128,640]{1,0:T(8,128)}, f32[128,640]{1,0:T(8,128)}, u32[]{:S(2)}, u32[]{:S(2)}) collective-permute-start(f32[128,640]{1,0:T(8,128)} %get-tuple-element.35), channel_id=1, source_target_pairs={{0,1},{1,0},{2,3},{3,2},{4,5},{5,4},{6,7},{7,6},{8,9},{9,8},{10,11... | collective-permute-start | bytes 983048 | tf_op jit(solution)/shard_map/ppermute | solution.py:44
  73.1 12.2 %all-to-all-start.3 = ((f32[8,40,128]{2,1,0:T(8,128)}), f32[8,40,128]{2,1,0:T(8,128)S(1)}, u32[]{:S(2)}, u32[]{:S(2)}) async-start(f32[8,40,128]{2,1,0:T(8,128)} %copy-done.11), calls=%async_computation.3 | async-start | bytes 327680 | tf_op jit(solution)/shard_map/all_to_all | solution.py:394
  78.0 53.5 %collective-permute-start.12 = (f32[128,640]{1,0:T(8,128)}, f32[128,640]{1,0:T(8,128)}, u32[]{:S(2)}, u32[]{:S(2)}) collective-permute-start(f32[128,640]{1,0:T(8,128)} %copy-done.4), channel_id=1, source_target_pairs={{16,0},{17,1},{18,2},{19,3},{20,4},{21,5},{22,6},{23,7},{24,8},{25... | collective-permute-start | bytes 983048 | tf_op jit(solution)/shard_map/ppermute | solution.py:63
  79.3 13.7 %collective-permute-start.2 = (f32[128,640]{1,0:T(8,128)}, f32[128,640]{1,0:T(8,128)S(1)}, u32[]{:S(2)}, u32[]{:S(2)}) collective-permute-start(f32[128,640]{1,0:T(8,128)} %copy-done.7), channel_id=1, source_target_pairs={{0,16},{1,17},{2,18},{3,19},{4,20},{5,21},{6,22},{7,23},{8,24},{9,... | collective-permute-start | bytes 983048 | tf_op jit(solution)/shard_map/ppermute | solution.py:63
  84.7 10.9 %collective-permute-start.1 = (f32[128,640]{1,0:T(8,128)}, f32[128,640]{1,0:T(8,128)}, u32[]{:S(2)}, u32[]{:S(2)}) collective-permute-start(f32[128,640]{1,0:T(8,128)} %copy-done.20), channel_id=1, source_target_pairs={{0,1},{1,0},{2,3},{3,2},{4,5},{5,4},{6,7},{7,6},{8,9},{9,8},{10,11... | collective-permute-start | bytes 983048 | tf_op jit(solution)/shard_map/ppermute | solution.py:44
  85.8 15.8 %collective-permute-start.7 = (f32[128,640]{1,0:T(8,128)S(1)}, f32[128,640]{1,0:T(8,128)}, u32[]{:S(2)}, u32[]{:S(2)}) collective-permute-start(f32[128,640]{1,0:T(8,128)S(1)} %shard_map.146), channel_id=1, source_target_pairs={{0,1},{1,0},{2,3},{3,2},{4,5},{5,4},{6,7},{7,6},{8,9},{9,8},{10,11... | collective-permute-start | bytes 983048 | tf_op jit(solution)/shard_map/ppermute | solution.py:44
  89.2 22.1 %collective-permute-start.4 = (f32[128,640]{1,0:T(8,128)}, f32[128,640]{1,0:T(8,128)}, u32[]{:S(2)}, u32[]{:S(2)}) collective-permute-start(f32[128,640]{1,0:T(8,128)} %add.131), channel_id=1, source_target_pairs={{0,16},{16,0},{1,17},{17,1},{2,18},{18,2},{3,19},{19,3},{4,20},{20... | collective-permute-start | bytes 983048 | tf_op jit(solution)/shard_map/ppermute | solution.py:63
  94.0 37.5 %collective-permute-start.11 = (f32[128,640]{1,0:T(8,128)}, f32[128,640]{1,0:T(8,128)S(1)}, u32[]{:S(2)}, u32[]{:S(2)}) collective-permute-start(f32[128,640]{1,0:T(8,128)} %copy-done.19), channel_id=1, source_target_pairs={{16,0},{17,1},{18,2},{19,3},{20,4},{21,5},{22,6},{23,7},{24,8},{25... | collective-permute-start | bytes 983048 | tf_op jit(solution)/shard_map/ppermute | solution.py:63
  110.7 19.1 %collective-permute-start.8 = (f32[64,640]{1,0:T(8,128)S(1)}, f32[64,640]{1,0:T(8,128)S(1)}, u32[]{:S(2)}, u32[]{:S(2)}) collective-permute-start(f32[64,640]{1,0:T(8,128)S(1)} %get-tuple-element.42), channel_id=1, source_target_pairs={{0,1},{1,0},{2,3},{3,2},{4,5},{5,4},{6,7},{7,6},{8,9},{9,8},{10,11... | collective-permute-start | bytes 491528 | tf_op jit(solution)/shard_map/ppermute | solution.py:44
  112.4 19.1 %copy-start.6 = (f32[128,640]{1,0:T(8,128)S(1)}, f32[128,640]{1,0:T(8,128)}, u32[]{:S(2)}) copy-start(f32[128,640]{1,0:T(8,128)} %copy-done.4) | copy-start | bytes 983044
  120.0 18.8 %copy-start.3 = (f32[1,64,640]{2,1,0:T(8,128)S(1)}, f32[1,64,640]{2,1,0:T(8,128)}, u32[]{:S(2)}) copy-start(f32[1,64,640]{2,1,0:T(8,128)} %param.13) | copy-start | bytes 491524
  120.0 18.8 %copy-start.8 = (f32[128,640]{1,0:T(8,128)S(1)}, f32[128,640]{1,0:T(8,128)}, u32[]{:S(2)}) copy-start(f32[128,640]{1,0:T(8,128)} %copy-done.7) | copy-start | bytes 983044
  120.0 18.8 %copy-start.10 = (f32[128,64]{1,0:T(8,128)S(1)}, f32[128,64]{1,0:T(8,128)}, u32[]{:S(2)}) copy-start(f32[128,64]{1,0:T(8,128)} %copy-done.9) | copy-start | bytes 98308
  120.0 8.5 %collective-permute-start.5 = (f32[128,640]{1,0:T(8,128)S(1)}, f32[128,640]{1,0:T(8,128)S(1)}, u32[]{:S(2)}, u32[]{:S(2)}) collective-permute-start(f32[128,640]{1,0:T(8,128)S(1)} %get-tuple-element.38), channel_id=1, source_target_pairs={{0,1},{1,0},{2,3},{3,2},{4,5},{5,4},{6,7},{7,6},{8,9},{9,8},{10,11... | collective-permute-start | bytes 983048 | tf_op jit(solution)/shard_map/ppermute | solution.py:44
  121.7 17.1 %collective-permute-start.10 = (f32[128,640]{1,0:T(8,128)S(1)}, f32[128,640]{1,0:T(8,128)S(1)}, u32[]{:S(2)}, u32[]{:S(2)}) collective-permute-start(f32[128,640]{1,0:T(8,128)S(1)} %pad_maximum_fusion.1), channel_id=1, source_target_pairs={{16,0},{17,1},{18,2},{19,3},{20,4},{21,5},{22,6},{23,7},{24,8},{25... | collective-permute-start | bytes 983048 | tf_op jit(solution)/shard_map/ppermute | solution.py:63
  128.5 10.2 %collective-permute-start.9 = (f32[128,640]{1,0:T(8,128)S(1)}, f32[128,640]{1,0:T(8,128)S(1)}, u32[]{:S(2)}, u32[]{:S(2)}) collective-permute-start(f32[128,640]{1,0:T(8,128)S(1)} %add.134.refs_0_), channel_id=1, source_target_pairs={{16,0},{17,1},{18,2},{19,3},{20,4},{21,5},{22,6},{23,7},{24,8},{25... | collective-permute-start | bytes 983048 | tf_op jit(solution)/shard_map/ppermute | solution.py:63
  129.9 14.1 %collective-permute-start.13 = (f32[64,640]{1,0:T(8,128)S(1)}, f32[64,640]{1,0:T(8,128)S(1)}, u32[]{:S(2)}, u32[]{:S(2)}) collective-permute-start(f32[64,640]{1,0:T(8,128)S(1)} %get-tuple-element.48.moved_ref.moved_state_ref), channel_id=1, source_target_pairs={{0,1},{1,0},{2,3},{3,2},{4,5},{5,4},{6,7},{7,6},{8,9},{9,8},{10,11... | collective-permute-start | bytes 491528 | tf_op jit(solution)/shard_map/ppermute | solution.py:44
  140.6 10.6 %all-to-all-start.4 = ((f32[32,1,128]{2,1,0:T(1,128)}), f32[32,1,128]{2,1,0:T(1,128)S(1)}, u32[]{:S(2)}, u32[]{:S(2)}) async-start(f32[32,1,128]{2,1,0:T(1,128)} %bitcast.17), calls=%async_computation.4 | async-start | bytes 32768 | tf_op jit(solution)/shard_map/all_to_all | solution.py:514
  (10 other events, 7.3 us)
